TPU v7x, 128 devices: a whole 4x4x4 slice. The times are simulated.
128 devices in a mesh: expert: 32 (over y, z, core), rep: 4 (over x).
Axes of the slice: x: 4, y: 4, z: 4, core: 2. Of those that a mesh axis runs over, the one named last changes fastest.
Arguments:
- tokens: bfloat16 [16384, 1664], P(('expert', 'rep')), may hold values from -50 to 50
- grad_grid: bfloat16 [256, 256, 1664], P(('expert', 'rep')), may hold values from -18 to 18
- keep_order: int32 [256, 256], P(('expert', 'rep')), may hold values from 0 to 255, each once within a row
- expert_ids: int32 [16384, 2], P(('expert', 'rep')), may hold values from 0 to 31, all different within a row; in each aligned block of 128 rows (0 to 127, 128 to 255, ...) at most 10 rows name the same one
- norm_gain: float32 [1664], replicated, may hold values from 0.25 to 1.75
- norm_bias: float32 [1664], replicated, may hold values from -3 to 3
- router_weight: float32 [1664, 32], replicated, may hold values from -0.15625 to 0.15625
- w_in: bfloat16 [32, 1664, 4096], P('expert', None, 'rep'), may hold values from -0.15625 to 0.15625
- w_out: bfloat16 [32, 4096, 1664], P('expert', 'rep'), may hold values from -0.09375 to 0.09375
Outputs:
- grad_tokens: bfloat16 [16384, 1664], P(('expert', 'rep'))
- grad_w_in: float32 [32, 1664, 4096], P('expert', None, 'rep')
- grad_w_out: float32 [32, 4096, 1664], P('expert', 'rep')
- grad_router: float32 [1664, 32], replicated
- grad_gain: float32 [1664], replicated
- grad_bias: float32 [1664], replicated
Inputs may be any that keep to these rules, and one draw needn't show every extreme that they name: `expert_ids`: each row names two different experts. Within the 128 rows of one device (aligned blocks) no expert is named more than 10 times, a bound that some block reaches. `keep_order`: each row is an order of the 256 patches of its image; its first 64 entries are the kept patches, in the order of the image's kept tokens.
All inputs are finite; a program needn't handle non-finite values.
Results may differ from a plain program's by a relative error of at most 0.0062.
Values may be sent and summed in bfloat16 or wider, within the bound.
A program may use at most 128 MiB of HBM per device.

v0:
```python
import jax
import jax.numpy as jnp
from jax import lax
from jax.sharding import PartitionSpec as P

NORM_EPS = 1e-06
PRECISE = lax.Precision.HIGHEST


def gelu_parts(preact):
    normal_cdf = 0.5 * (1.0 + lax.erf(preact * 0.7071067811865476))
    density = jnp.exp(-0.5 * preact * preact) * 0.3989422804014327
    return (preact * normal_cdf, normal_cdf + preact * density)


def contract(left, right, left_axis, right_axis):
    return lax.dot_general(
        left, right, (((left_axis,), (right_axis,)), ((), ())), preferred_element_type=jnp.float32
    )


def layer_norm(tokens, norm_gain, norm_bias):
    values = tokens.astype(jnp.float32)
    center = values - jnp.mean(values, axis=1, keepdims=True)
    inverse = 1.0 / jnp.sqrt(jnp.mean(center * center, axis=1, keepdims=True) + NORM_EPS)
    normed = center * inverse
    return (normed, inverse, (normed * norm_gain + norm_bias).astype(jnp.bfloat16))


def gate_values(normed_in, router_weight, expert_ids):
    experts = router_weight.shape[1]
    logits = jnp.dot(normed_in.astype(jnp.float32), router_weight, precision=PRECISE)
    chosen = (expert_ids[:, :, None] == jnp.arange(experts, dtype=jnp.int32)[None, None, :]).astype(
        jnp.float32
    )
    picked = jnp.sum(logits[:, None, :] * chosen, axis=2)
    first_gate = jax.nn.sigmoid(picked[:, 0] - picked[:, 1])
    second_gate = jax.nn.sigmoid(picked[:, 1] - picked[:, 0])
    return (chosen, first_gate, second_gate)


def expert_rows(normed_rows, grad_rows, gate_rows, weight_in, weight_out):
    preact = contract(normed_rows, weight_in, 1, 0)
    hidden, hidden_slope = gelu_parts(preact)
    gate_col = gate_rows.astype(jnp.float32)[:, None]
    weighted = (gate_col * hidden).astype(jnp.bfloat16)
    back_hidden = contract(grad_rows, weight_out, 1, 1)
    gate_grad = jnp.sum(back_hidden * hidden, axis=1)
    pre_grad = (gate_col * back_hidden * hidden_slope).astype(jnp.bfloat16)
    grad_out = contract(weighted, grad_rows, 0, 0)
    grad_in = contract(normed_rows, pre_grad, 0, 0)
    input_grad = contract(pre_grad, weight_in, 1, 1)
    return (input_grad, gate_grad, grad_in, grad_out)


def on_device(
    tokens, grad_grid, keep_order, expert_ids, norm_gain, norm_bias, router_weight, w_in, w_out
):
    experts = router_weight.shape[1]
    local_count = w_in.shape[0]
    groups = lax.axis_size("expert")
    copies = lax.axis_size("rep")
    tok_count = tokens.shape[0]
    model_width = tokens.shape[1]
    capacity = 5 * tok_count // (2 * experts)
    kept_count = tok_count // grad_grid.shape[0]
    grad_kept = jnp.take_along_axis(grad_grid, keep_order[:, :kept_count, None], axis=1).reshape(
        tok_count, model_width
    )
    normed, inverse, normed_in = layer_norm(tokens, norm_gain, norm_bias)
    chosen, first_gate, second_gate = gate_values(normed_in, router_weight, expert_ids)
    gate_half = jnp.stack([first_gate, second_gate], axis=1).astype(jnp.bfloat16)
    expert_hits = jnp.sum(chosen, axis=1)
    before = jnp.cumsum(expert_hits, axis=0) - expert_hits
    slot_place = jnp.sum(before[:, None, :] * chosen, axis=2).astype(jnp.int32)
    slot_index = expert_ids * capacity + slot_place
    slot_ids = jnp.arange(experts * capacity, dtype=jnp.int32)
    spread = (slot_index[:, :, None] == slot_ids[None, None, :]).astype(jnp.float32)
    assign = jnp.sum(spread, axis=1)
    assign_half = assign.astype(jnp.bfloat16)
    send_normed = (
        contract(assign_half, normed_in, 0, 0)
        .astype(jnp.bfloat16)
        .reshape(experts, capacity, model_width)
    )
    send_grad = (
        contract(assign_half, grad_kept, 0, 0)
        .astype(jnp.bfloat16)
        .reshape(experts, capacity, model_width)
    )
    send_gate = (
        jnp.einsum("tks,tk->s", spread, gate_half.astype(jnp.float32), precision=PRECISE)
        .astype(jnp.bfloat16)
        .reshape(experts, capacity)
    )

    def widen(part):
        tail = part.shape[1:]
        grown = jnp.broadcast_to(
            part.reshape((groups, 1, local_count) + tail), (groups, copies, local_count) + tail
        )
        return grown.reshape((groups * copies * local_count,) + tail)

    got_normed, got_grad, got_gate = (
        lax.all_to_all(
            widen(send_normed), ("expert", "rep"), split_axis=0, concat_axis=0, tiled=True
        ),
        lax.all_to_all(
            widen(send_grad), ("expert", "rep"), split_axis=0, concat_axis=0, tiled=True
        ),
        lax.all_to_all(
            widen(send_gate), ("expert", "rep"), split_axis=0, concat_axis=0, tiled=True
        ),
    )
    row_parts, gate_parts, in_parts, out_parts = ([], [], [], [])

    def pick_rows(part):
        return part.reshape((groups, copies, local_count) + part.shape[1:])[:, :, 0].reshape(
            (-1,) + part.shape[2:]
        )

    input_grad, gate_grad, grad_in, grad_out = expert_rows(
        pick_rows(got_normed), pick_rows(got_grad), pick_rows(got_gate), w_in[0], w_out[0]
    )
    row_parts.append(input_grad.reshape(groups, copies, 1, capacity, model_width))
    gate_parts.append(gate_grad.reshape(groups, copies, 1, capacity))
    in_parts.append(grad_in)
    out_parts.append(grad_out)
    back_rows, back_gate = (
        lax.psum_scatter(row_parts[0], "rep", scatter_dimension=1, tiled=True),
        lax.psum_scatter(gate_parts[0], "rep", scatter_dimension=1, tiled=True),
    )
    grad_w_in = jnp.stack(in_parts)
    grad_w_out = jnp.stack(out_parts)
    ret_rows, ret_gate = (
        lax.all_to_all(
            back_rows.reshape(experts, capacity, model_width),
            "expert",
            split_axis=0,
            concat_axis=0,
            tiled=True,
        ),
        lax.all_to_all(
            back_gate.reshape(experts, capacity), "expert", split_axis=0, concat_axis=0, tiled=True
        ),
    )
    mixed_grad = jnp.dot(
        assign, ret_rows.reshape(experts * capacity, model_width), precision=PRECISE
    )
    gate_grads = jnp.einsum(
        "tks,s->tk", spread, ret_gate.reshape(experts * capacity), precision=PRECISE
    )
    logit_grad = first_gate * second_gate * (gate_grads[:, 0] - gate_grads[:, 1])
    logits_grad = logit_grad[:, None] * (chosen[:, 0] - chosen[:, 1])
    normed_grad = mixed_grad + lax.dot_general(
        logits_grad, router_weight, (((1,), (1,)), ((), ())), precision=PRECISE
    )
    local_router = lax.dot_general(
        normed_in.astype(jnp.float32), logits_grad, (((0,), (0,)), ((), ())), precision=PRECISE
    )
    local_gain = jnp.sum(normed_grad * normed, axis=0)
    local_bias = jnp.sum(normed_grad, axis=0)
    grad_router, grad_gain, grad_bias = lax.psum(
        (local_router, local_gain, local_bias), ("expert", "rep")
    )
    scaled = normed_grad * norm_gain
    branch = inverse * (
        scaled
        - jnp.mean(scaled, axis=1, keepdims=True)
        - normed * jnp.mean(scaled * normed, axis=1, keepdims=True)
    )
    grad_tokens = (grad_kept.astype(jnp.float32) + branch).astype(jnp.bfloat16)
    return (grad_tokens, grad_w_in, grad_w_out, grad_router, grad_gain, grad_bias)


def solution(mesh):
    placed = (
        P(("expert", "rep"), None),
        P(("expert", "rep"), None, None),
        P(("expert", "rep"), None),
        P(("expert", "rep"), None),
        P(),
        P(),
        P(),
        P("expert", None, "rep"),
        P("expert", "rep", None),
    )
    return jax.shard_map(
        on_device,
        mesh=mesh,
        in_specs=placed,
        out_specs=(
            P(("expert", "rep"), None),
            P("expert", None, "rep"),
            P("expert", "rep", None),
            P(),
            P(),
            P(),
        ),
        check_vma=False,
    )
```

profile of v0, /device:TPU:1, one launch (start us, length us, event | category | flops | bytes accessed | tf_op | source)
XLA Modules:
  0.0 523.4 jit_solution(1919099164232405682)
XLA Ops:
  18.8 2.4 convolution_convert_fusion
  21.2 2.4 broadcast_in_dim.59
  23.6 4.8 broadcast_in_dim.60
  28.4 11.9 %all-to-all-start.2 = ((bf16[128,10,1664]{2,1,0:T(8,128)(2,1)}), bf16[128,10,1664]{2,1,0:T(8,128)(2,1)}, u32[]{:S(2)}, u32[]{:S(2)}) async-start(bf16[128,10,1664]{2,1,0:T(8,128)(2,1)} %bitcast.60), calls=%async_computation.2 | async-start | bytes 13631488 | tf_op jit(solution)/shard_map/all_to_all | solution.py:105
  40.5 3.3 gather_fusion
  43.8 2.6 convolution_convert_fusion.1
  46.4 2.4 broadcast_in_dim.56
  48.8 74.0 %all-to-all-done.2 = bf16[128,10,1664]{2,1,0:T(8,128)(2,1)} async-done(((bf16[128,10,1664]{2,1,0:T(8,128)(2,1)}), bf16[128,10,1664]{2,1,0:T(8,128)(2,1)}, u32[]{:S(2)}, u32[]{:S(2)}) %all-to-all-start.2) | async-done | bytes 4259872 | tf_op jit(solution)/shard_map/all_to_all | solution.py:105
  122.8 4.8 broadcast_in_dim.57
  127.6 7.8 %all-to-all-start.1 = ((bf16[128,10,1664]{2,1,0:T(8,128)(2,1)}), bf16[128,10,1664]{2,1,0:T(8,128)(2,1)}, u32[]{:S(2)}, u32[]{:S(2)}) async-start(bf16[128,10,1664]{2,1,0:T(8,128)(2,1)} %bitcast.59), calls=%async_computation.1 | async-start | bytes 13631488 | tf_op jit(solution)/shard_map/all_to_all | solution.py:108
  136.1 7.7 %reshape_squeeze_reshape.8 = bf16[1280,1664]{1,0:T(8,128)(2,1)} reshape(bf16[128,10,1664]{2,1,0:T(8,128)(2,1)} %all-to-all-done.2) | data formatting | bytes 8519680 | tf_op jit(solution)/shard_map/reshape;squeeze;reshape | solution.py:118
  143.9 8.9 %fusion.7 = f32[1280,1024]{1,0:T(8,128)} fusion(bf16[1280,1664]{1,0:T(8,128)(2,1)} %reshape_squeeze_reshape.8, bf16[1,1664,1024]{2,1,0:T(8,128)(2,1)S(1)} %copy-done), kind=kOutput, calls=%fused_computation.15 | convolution fusion | flops 4362076160 | bytes 12910592 | tf_op jit(solution)/shard_map/dot_general | solution.py:17
  152.8 65.2 %all-to-all-done.1 = bf16[128,10,1664]{2,1,0:T(8,128)(2,1)} async-done(((bf16[128,10,1664]{2,1,0:T(8,128)(2,1)}), bf16[128,10,1664]{2,1,0:T(8,128)(2,1)}, u32[]{:S(2)}, u32[]{:S(2)}) %all-to-all-start.1) | async-done | bytes 4259872 | tf_op jit(solution)/shard_map/all_to_all | solution.py:108
  218.0 7.7 %reshape_squeeze_reshape.7 = bf16[1280,1664]{1,0:T(8,128)(2,1)} reshape(bf16[128,10,1664]{2,1,0:T(8,128)(2,1)} %all-to-all-done.1) | data formatting | bytes 8519680 | tf_op jit(solution)/shard_map/reshape;squeeze;reshape | solution.py:118
  225.7 10.8 %multiply_reduce_fusion = (f32[1280]{0:T(1024)S(1)}, f32[1280,1024]{1,0:T(8,128)}) fusion(f32[1280,1024]{1,0:T(8,128)} %fusion.7, bf16[1280,1664]{1,0:T(8,128)(2,1)} %reshape_squeeze_reshape.7, bf16[1,1024,1664]{2,1,0:T(8,128)(2,1)} %param.17), kind=kOutput, calls=%fused_computation.9 | convolution fusion | flops 4369939456 | bytes 18158592 | tf_op jit(solution)/shard_map/dot_general | solution.py:17
  236.8 13.0 %all-reduce = f32[32,4,1,10]{0,2,3,1:T(1,128)S(1)} all-reduce(f32[32,4,1,10]{0,2,3,1:T(1,128)S(1)} %copy.45), channel_id=3, replica_groups=mesh['expert'=32,'rep'=4] {'rep'}, use_global_device_ids=true, to_apply=%region_9.10.clone | all-reduce | flops 1280 | bytes 10240
  250.5 16.6 %all_to_all.33 = f32[32,1,10]{2,1,0:T(1,128)S(1)} all-to-all(f32[32,1,10]{2,1,0:T(1,128)S(1)} %copy.46), channel_id=1, replica_groups=mesh['expert'=32,'rep'=4] {'expert'}, dimensions={0} | all-to-all | bytes 2560 | tf_op jit(solution)/shard_map/all_to_all | solution.py:143
  269.0 14.0 %all_to_all.34 = bf16[128,1,10]{2,1,0:T(2,128)(2,1)S(1)} all-to-all(bf16[128,1,10]{2,1,0:T(2,128)(2,1)S(1)} %copy.42), channel_id=1, replica_groups=mesh['expert'=32,'rep'=4] {'expert','rep'}, dimensions={0} | all-to-all | bytes 5120 | tf_op jit(solution)/shard_map/all_to_all | solution.py:111
  283.3 6.5 %fusion.5 = bf16[1280,1024]{1,0:T(8,128)(2,1)} fusion(f32[1280,1024]{1,0:T(8,128)} %fusion.7, f32[1280,1024]{1,0:T(8,128)} %get-tuple-element.18, f32[1280]{0:T(1024)S(1)} %reshape.115), kind=kLoop, calls=%fused_computation.7 | loop fusion | flops 14417920 | bytes 13112320 | tf_op jit(solution)/shard_map/convert_element_type | solution.py:49
  289.8 5.9 %reshape.110 = bf16[32,4,10,1024]{3,2,1,0:T(8,128)(2,1)} reshape(bf16[1280,1024]{1,0:T(8,128)(2,1)} %fusion.5) | data formatting | bytes 5242880 | tf_op jit(solution)/shard_map/reshape.66
  295.7 11.7 %convolution_bitcast_fusion = f32[32,4,1,10,1664]{4,0,3,1,2:T(8,128)} fusion(bf16[1,1664,1024]{2,1,0:T(8,128)(2,1)S(1)} %copy-done, bf16[32,4,10,1024]{3,2,1,0:T(8,128)(2,1)} %reshape.110), kind=kOutput, calls=%fused_computation.11 | convolution fusion | flops 4362076160 | bytes 14548992 | tf_op jit(solution)/shard_map/dot_general | solution.py:17
  308.1 2.0 fusion.40
  310.1 75.4 %reduce-scatter.2.cloned.1.call-done = f32[32,1,1,10,1664]{4,0,3,1,2:T(8,128)} async-done(((f32[32,4,1,10,1664]{4,0,3,1,2:T(8,128)}), f32[32,1,1,10,1664]{4,0,3,1,2:T(8,128)}) %reduce-scatter.2.cloned.1.call-update) | async-done | bytes 2129936 | tf_op jit(solution)/shard_map/reduce_scatter | solution.py:130
  385.6 4.7 copy.44
  390.2 7.6 %all-to-all-start.3 = ((f32[32,10,1664]{2,1,0:T(8,128)}), f32[32,10,1664]{2,1,0:T(8,128)}, u32[]{:S(2)}, u32[]{:S(2)}) async-start(f32[32,10,1664]{2,1,0:T(8,128)} %copy.44), calls=%async_computation.4 | async-start | bytes 6815744 | tf_op jit(solution)/shard_map/all_to_all | solution.py:136
  397.9 10.7 %convolution_bitcast_fusion.2 = f32[1,1664,1024]{2,1,0:T(8,128)} fusion(bf16[1280,1664]{1,0:T(8,128)(2,1)} %reshape_squeeze_reshape.8, bf16[1280,1024]{1,0:T(8,128)(2,1)} %fusion.5), kind=kOutput, calls=%fused_computation.13 | convolution fusion | flops 4362076160 | bytes 13697024 | tf_op jit(solution)/shard_map/dot_general | solution.py:17
  408.5 9.0 %convolution_bitcast_fusion.1 = f32[1,1024,1664]{2,1,0:T(8,128)} fusion(bf16[1280,1664]{1,0:T(8,128)(2,1)S(1)} %bitcast.62, f32[1280]{0:T(1024)S(1)} %reshape.115, f32[1280,1024]{1,0:T(8,128)} %fusion.7), kind=kOutput, calls=%fused_computation.12 | convolution fusion | flops 4369940480 | bytes 16323584 | tf_op jit(solution)/shard_map/dot_general | solution.py:17
  417.5 23.0 %all-to-all-done.3 = f32[32,10,1664]{2,1,0:T(8,128)} async-done(((f32[32,10,1664]{2,1,0:T(8,128)}), f32[32,10,1664]{2,1,0:T(8,128)}, u32[]{:S(2)}, u32[]{:S(2)}) %all-to-all-start.3) | async-done | bytes 2129952 | tf_op jit(solution)/shard_map/all_to_all | solution.py:136
  440.5 3.1 reshape.112
  443.7 3.5 fusion.46
  447.1 2.3 fusion.27
  450.7 63.7 %all-reduce.1 = (f32[1664]{0:T(1024)}, f32[1664]{0:T(1024)}) all-reduce(f32[1664]{0:T(1024)S(1)} %get-tuple-element.6, f32[1664]{0:T(1024)S(1)} %get-tuple-element.9), channel_id=1, replica_groups=mesh['expert'=32,'rep'=4] {'expert','rep'}, use_global_device_ids=true, to_apply=%region_14.15 | all-reduce | flops 3328 | bytes 26624 | tf_op jit(solution)/shard_map/psum | solution.py:163
  (67 shorter events, 18.3 us)
Async XLA Ops:
  8.0 135.9 %copy-start = (bf16[1,1664,1024]{2,1,0:T(8,128)(2,1)S(1)}, bf16[1,1664,1024]{2,1,0:T(8,128)(2,1)}, u32[]{:S(2)}) copy-start(bf16[1,1664,1024]{2,1,0:T(8,128)(2,1)} %param.16) | copy-start | bytes 10223620
  12.0 0.8 copy-start.2
  18.1 0.7 copy-start.4
  28.4 11.9 %copy-start.7 = (s32[2,256]{1,0:T(2,128)S(1)}, s32[2,256]{1,0:T(2,128)}, u32[]{:S(2)}) copy-start(s32[2,256]{1,0:T(2,128)} %param.11) | copy-start | bytes 6148
  28.4 94.4 %all-to-all-start.2 = ((bf16[128,10,1664]{2,1,0:T(8,128)(2,1)}), bf16[128,10,1664]{2,1,0:T(8,128)(2,1)}, u32[]{:S(2)}, u32[]{:S(2)}) async-start(bf16[128,10,1664]{2,1,0:T(8,128)(2,1)} %bitcast.60), calls=%async_computation.2 | async-start | bytes 13631488 | tf_op jit(solution)/shard_map/all_to_all | solution.py:105
  127.6 7.9 %copy-start.8 = (u32[128]{0:T(128)S(1)}, u32[128]{0:T(128)}, u32[]{:S(2)}) copy-start(u32[128]{0:T(128)} %constant.62) | copy-start | bytes 1540
  127.6 90.4 %all-to-all-start.1 = ((bf16[128,10,1664]{2,1,0:T(8,128)(2,1)}), bf16[128,10,1664]{2,1,0:T(8,128)(2,1)}, u32[]{:S(2)}, u32[]{:S(2)}) async-start(bf16[128,10,1664]{2,1,0:T(8,128)(2,1)} %bitcast.59), calls=%async_computation.1 | async-start | bytes 13631488 | tf_op jit(solution)/shard_map/all_to_all | solution.py:108
  135.5 250.1 %reduce-scatter.2.cloned.1.call-start = ((), (), s32[]{:S(2)}) async-start(), calls=%async_computation.6 | async-start | bytes 10649600 | tf_op jit(solution)/shard_map/reduce_scatter | solution.py:130
  307.4 0.7 copy-start.6
  307.4 206.9 %all-reduce.4.cloned.1.call-start = ((), (), s32[]{:S(2)}) async-start(), calls=%async_computation.7 | async-start | bytes 425984 | tf_op jit(solution)/shard_map/psum | solution.py:163
  390.2 18.3 %slice-start = ((s8[4259840]{0:T(1024)(128)(4,1)}), s8[65536]{0:T(1024)(128)(4,1)S(1)}, s32[]{:S(2)}) async-start(s8[4259840]{0:T(1024)(128)(4,1)} %bitcast.61), calls=%async_computation.8 | async-start | bytes 131072
  390.2 50.3 %all-to-all-start.3 = ((f32[32,10,1664]{2,1,0:T(8,128)}), f32[32,10,1664]{2,1,0:T(8,128)}, u32[]{:S(2)}, u32[]{:S(2)}) async-start(f32[32,10,1664]{2,1,0:T(8,128)} %copy.44), calls=%async_computation.4 | async-start | bytes 6815744 | tf_op jit(solution)/shard_map/all_to_all | solution.py:136
  397.8 10.7 %slice-start.1 = ((s8[4259840]{0:T(1024)(128)(4,1)}), s8[4194304]{0:T(1024)(128)(4,1)S(1)}, s32[]{:S(2)}) async-start(s8[4259840]{0:T(1024)(128)(4,1)} %bitcast.61), calls=%async_computation.9 | async-start | bytes 8388608
  417.5 29.6 %copy-start.5 = (f32[1664]{0:T(1024)S(1)}, f32[1664]{0:T(1024)}, u32[]{:S(2)}) copy-start(f32[1664]{0:T(1024)} %param.13) | copy-start | bytes 19972
  443.7 5.8 %copy-start.1 = (bf16[128,1664]{1,0:T(8,128)(2,1)S(1)}, bf16[128,1664]{1,0:T(8,128)(2,1)}, u32[]{:S(2)}) copy-start(bf16[128,1664]{1,0:T(8,128)(2,1)} %param.9) | copy-start | bytes 1277956
  443.7 5.8 %copy-start.3 = (bf16[128,1664]{1,0:T(8,128)(2,1)S(1)}, bf16[128,1664]{1,0:T(8,128)(2,1)}, u32[]{:S(2)}) copy-start(bf16[128,1664]{1,0:T(8,128)(2,1)} %gather_fusion) | copy-start | bytes 1277956
Sparse Core Ops, SparseCore 0:
  307.6 77.9 reduce-scatter.1
Sparse Core Ops, SparseCore 1:
  313.3 198.9 all-reduce.3
where the time goes:
time: 525 us; the launch traced here: 523 us
  waiting for transfers between devices  238 us (45%)
  blocking collectives  107 us (20%)
  matrix products  65.7 us (13%)
  local copies, waits for them, and re-layouts  53.4 us (10%)
  starting transfers between devices  27.4 us (5%)
  other arithmetic  16.4 us (3%)
  between operations  15.7 us (3%)
    reduce_scatter x1, waiting for transfers between devices, on_device(): lax.psum_scatter(row_parts[0], 'rep', scatter_dimension=1, tiled=True)  75.4 us
    all_to_all x1, waiting for transfers between devices, on_device(): lax.all_to_all(widen(send_normed), ('expert', 'rep'), split_axis=0, conca...  74 us
    all_to_all x1, waiting for transfers between devices, on_device(): lax.all_to_all(widen(send_grad), ('expert', 'rep'), split_axis=0, concat_...  65.2 us
    psum x1, blocking collectives, on_device(): lax.psum((local_router, local_gain, local_bias), ('expert', 'rep'))  63.7 us
    dot_general x7, matrix products, contract(): lax.dot_general(left, right, (((left_axis,), (right_axis,)), ((), ())), p...  56 us
    all_to_all x1, waiting for transfers between devices, on_device(): lax.all_to_all(back_rows.reshape(experts, capacity, model_width), 'expert...  23 us
    all_to_all x1, blocking collectives, on_device(): lax.all_to_all(back_gate.reshape(experts, capacity), 'expert', split_axis...  16.6 us
    another operation x2, local copies, waits for them, and re-layouts, pick_rows(): part.reshape((groups, copies, local_count) + part.shape[1:])[:, :, 0]  15.5 us
  transfers between devices with their start and end apart: 5, of which 4 were waited for; matrix products, arithmetic and copies ran while one was open for 12% of the time, Pallas kernels for 0%

commit v1 on v0

--- a/solution.py
+++ b/solution.py
@@ -57,13 +57,11 @@
     tokens, grad_grid, keep_order, expert_ids, norm_gain, norm_bias, router_weight, w_in, w_out
 ):
     experts = router_weight.shape[1]
-    local_count = w_in.shape[0]
-    groups = lax.axis_size("expert")
-    copies = lax.axis_size("rep")
     tok_count = tokens.shape[0]
     model_width = tokens.shape[1]
     capacity = 5 * tok_count // (2 * experts)
     kept_count = tok_count // grad_grid.shape[0]
+    lane = 128
     grad_kept = jnp.take_along_axis(grad_grid, keep_order[:, :kept_count, None], axis=1).reshape(
         tok_count, model_width
     )
@@ -78,78 +76,41 @@
     spread = (slot_index[:, :, None] == slot_ids[None, None, :]).astype(jnp.float32)
     assign = jnp.sum(spread, axis=1)
     assign_half = assign.astype(jnp.bfloat16)
-    send_normed = (
-        contract(assign_half, normed_in, 0, 0)
-        .astype(jnp.bfloat16)
-        .reshape(experts, capacity, model_width)
+    both = jnp.concatenate([normed_in, grad_kept], axis=1)
+    send_rows = contract(assign_half, both, 0, 0).astype(jnp.bfloat16)
+    send_gate = jnp.einsum(
+        "tks,tk->s", spread, gate_half.astype(jnp.float32), precision=PRECISE
+    ).astype(jnp.bfloat16)
+    gate_block = jnp.concatenate(
+        [send_gate[:, None], jnp.zeros((experts * capacity, lane - 1), jnp.bfloat16)], axis=1
     )
-    send_grad = (
-        contract(assign_half, grad_kept, 0, 0)
-        .astype(jnp.bfloat16)
-        .reshape(experts, capacity, model_width)
+    send = jnp.concatenate([send_rows, gate_block], axis=1).reshape(experts, capacity, -1)
+    got = lax.all_to_all(send, "expert", split_axis=0, concat_axis=0, tiled=True)
+    got = lax.all_gather(got, "rep", axis=0, tiled=True)
+    got = got.reshape(-1, got.shape[-1])
+    input_grad, gate_grad, grad_in, grad_out = expert_rows(
+        got[:, :model_width],
+        got[:, model_width : 2 * model_width],
+        got[:, 2 * model_width],
+        w_in[0],
+        w_out[0],
     )
-    send_gate = (
-        jnp.einsum("tks,tk->s", spread, gate_half.astype(jnp.float32), precision=PRECISE)
-        .astype(jnp.bfloat16)
-        .reshape(experts, capacity)
+    slots_all = input_grad.shape[0]
+    packed = jnp.concatenate(
+        [input_grad, gate_grad[:, None], jnp.zeros((slots_all, lane - 1), jnp.float32)], axis=1
     )
-
-    def widen(part):
-        tail = part.shape[1:]
-        grown = jnp.broadcast_to(
-            part.reshape((groups, 1, local_count) + tail), (groups, copies, local_count) + tail
-        )
-        return grown.reshape((groups * copies * local_count,) + tail)
-
-    got_normed, got_grad, got_gate = (
-        lax.all_to_all(
-            widen(send_normed), ("expert", "rep"), split_axis=0, concat_axis=0, tiled=True
-        ),
-        lax.all_to_all(
-            widen(send_grad), ("expert", "rep"), split_axis=0, concat_axis=0, tiled=True
-        ),
-        lax.all_to_all(
-            widen(send_gate), ("expert", "rep"), split_axis=0, concat_axis=0, tiled=True
-        ),
-    )
-    row_parts, gate_parts, in_parts, out_parts = ([], [], [], [])
-
-    def pick_rows(part):
-        return part.reshape((groups, copies, local_count) + part.shape[1:])[:, :, 0].reshape(
-            (-1,) + part.shape[2:]
-        )
-
-    input_grad, gate_grad, grad_in, grad_out = expert_rows(
-        pick_rows(got_normed), pick_rows(got_grad), pick_rows(got_gate), w_in[0], w_out[0]
-    )
-    row_parts.append(input_grad.reshape(groups, copies, 1, capacity, model_width))
-    gate_parts.append(gate_grad.reshape(groups, copies, 1, capacity))
-    in_parts.append(grad_in)
-    out_parts.append(grad_out)
-    back_rows, back_gate = (
-        lax.psum_scatter(row_parts[0], "rep", scatter_dimension=1, tiled=True),
-        lax.psum_scatter(gate_parts[0], "rep", scatter_dimension=1, tiled=True),
-    )
-    grad_w_in = jnp.stack(in_parts)
-    grad_w_out = jnp.stack(out_parts)
-    ret_rows, ret_gate = (
-        lax.all_to_all(
-            back_rows.reshape(experts, capacity, model_width),
-            "expert",
-            split_axis=0,
-            concat_axis=0,
-            tiled=True,
-        ),
-        lax.all_to_all(
-            back_gate.reshape(experts, capacity), "expert", split_axis=0, concat_axis=0, tiled=True
-        ),
-    )
-    mixed_grad = jnp.dot(
-        assign, ret_rows.reshape(experts * capacity, model_width), precision=PRECISE
-    )
-    gate_grads = jnp.einsum(
-        "tks,s->tk", spread, ret_gate.reshape(experts * capacity), precision=PRECISE
-    )
+    copies = lax.axis_size("rep")
+    packed = packed.reshape(copies, slots_all // copies, -1)
+    back = lax.psum_scatter(packed, "rep", scatter_dimension=0, tiled=True)
+    back = back.reshape(experts, capacity, -1)
+    ret = lax.all_to_all(back, "expert", split_axis=0, concat_axis=0, tiled=True)
+    ret = ret.reshape(experts * capacity, -1)
+    ret_rows = ret[:, :model_width]
+    ret_gate = ret[:, model_width]
+    grad_w_in = grad_in[None]
+    grad_w_out = grad_out[None]
+    mixed_grad = jnp.dot(assign, ret_rows, precision=PRECISE)
+    gate_grads = jnp.einsum("tks,s->tk", spread, ret_gate, precision=PRECISE)
     logit_grad = first_gate * second_gate * (gate_grads[:, 0] - gate_grads[:, 1])
     logits_grad = logit_grad[:, None] * (chosen[:, 0] - chosen[:, 1])
     normed_grad = mixed_grad + lax.dot_general(
@@ -160,9 +121,13 @@
     )
     local_gain = jnp.sum(normed_grad * normed, axis=0)
     local_bias = jnp.sum(normed_grad, axis=0)
-    grad_router, grad_gain, grad_bias = lax.psum(
-        (local_router, local_gain, local_bias), ("expert", "rep")
+    summed = lax.psum(
+        jnp.concatenate([local_router, local_gain[:, None], local_bias[:, None]], axis=1),
+        ("expert", "rep"),
     )
+    grad_router = summed[:, :experts]
+    grad_gain = summed[:, experts]
+    grad_bias = summed[:, experts + 1]
     scaled = normed_grad * norm_gain
     branch = inverse * (
         scaled

time: 525 us -> 564 us (1.074)
  waiting for transfers between devices: 238 us -> 338 us
  blocking collectives: 107 us -> 53.6 us
  starting transfers between devices: 27.4 us -> 8.35 us
  local copies, waits for them, and re-layouts: 53.4 us -> 71.1 us
    psum x1, waiting for transfers between devices: 0.01 us -> 139 us  [on_device(): lax.psum(jnp.concatenate([local_router, local_gain[:, None], local_bias[:...]
    all_to_all x3 -> x1, waiting for transfers between devices: 162 us -> 26.3 us  [on_device(): lax.all_to_all(back, 'expert', split_axis=0, concat_axis=0, tiled=True)]
    all_gather x0 -> x1, waiting for transfers between devices: none -> 83.8 us  [on_device(): got = lax.all_gather(got, 'rep', axis=0, tiled=True)]
    psum x1 -> x0, blocking collectives: 63.7 us -> none  [on_device(): lax.psum((local_router, local_gain, local_bias), ('expert', 'rep'))]
    concatenate x0 -> x5, local copies, waits for them, and re-layouts: none -> 23.2 us  [the longest x3 11.6 us: on_device(): jnp.concatenate([send_rows, gate_block], axis=1)]
    all_to_all x2 -> x1, blocking collectives: 30.6 us -> 53.6 us  [on_device(): lax.all_to_all(send, 'expert', split_axis=0, concat_axis=0, tiled=True)]
    another operation x3 -> x0, local copies, waits for them, and re-layouts: 21.4 us -> none  [the longest x2 15.5 us: pick_rows(): part.reshape((groups, copies, local_count) + part.shape[1:])[:, :, 0]]
    all_to_all x3 -> x1, starting transfers between devices: 27.3 us -> 7.83 us  [on_device(): lax.all_to_all(back, 'expert', split_axis=0, concat_axis=0, tiled=True)]
  transfers between devices with their start and end apart: 5 -> 4, of which waited for: 4 -> 4; matrix products, arithmetic and copies ran while one was open for 12% -> 4% of each run, Pallas kernels for 0% -> 0%
where the time goes in v1:
time: 564 us; the launch traced here: 562 us
  waiting for transfers between devices  338 us (60%)
  local copies, waits for them, and re-layouts  71.1 us (13%)
  matrix products  60.4 us (11%)
  blocking collectives  53.6 us (10%)
  other arithmetic  16.8 us (3%)
  between operations  14 us (2%)
  starting transfers between devices  8.35 us (1%)
    psum x1, waiting for transfers between devices, on_device(): lax.psum(jnp.concatenate([local_router, local_gain[:, None], local_bias[:...  139 us
    reduce_scatter x1, waiting for transfers between devices, on_device(): back = lax.psum_scatter(packed, 'rep', scatter_dimension=0, tiled=True)  88.1 us
    all_gather x1, waiting for transfers between devices, on_device(): got = lax.all_gather(got, 'rep', axis=0, tiled=True)  83.8 us
    all_to_all x1, blocking collectives, on_device(): lax.all_to_all(send, 'expert', split_axis=0, concat_axis=0, tiled=True)  53.6 us
    dot_general x6, matrix products, contract(): lax.dot_general(left, right, (((left_axis,), (right_axis,)), ((), ())), p...  50.2 us
    all_to_all x1, waiting for transfers between devices, on_device(): lax.all_to_all(back, 'expert', split_axis=0, concat_axis=0, tiled=True)  26.3 us
    reshape x1, local copies, waits for them, and re-layouts, on_device(): got = got.reshape(-1, got.shape[-1])  14.4 us
    all_gather x1, local copies, waits for them, and re-layouts, on_device(): got = lax.all_gather(got, 'rep', axis=0, tiled=True)  13.5 us
  transfers between devices with their start and end apart: 4, of which 4 were waited for; matrix products, arithmetic and copies ran while one was open for 4% of the time, Pallas kernels for 0%

profile of v1, /device:TPU:1, one launch (start us, length us, event | category | flops | bytes accessed | tf_op | source)
XLA Modules:
  0.0 561.9 jit_solution(3694275579578941825)
XLA Ops:
  10.6 1.3 fusion.34
  12.0 1.4 fusion.27
  14.1 1.5 fusion.55
  23.2 3.3 gather_fusion
  27.7 3.1 convolution_convert_fusion
  30.8 4.3 concatenate.21
  35.7 6.4 %concatenate.23 = bf16[32,10,3456]{2,1,0:T(8,128)(2,1)} concatenate(bf16[32,10,3328]{2,1,0:T(8,128)(2,1)} %concatenate.21, bf16[32,10,1]{2,1,0:T(8,128)(2,1)S(1)} %concatenate.30, bf16[32,10,127]{2,1,0:T(8,128)(2,1)} %broadcast_in_dim.25), dimensions={2} | concatenate | bytes 4423680 | tf_op jit(solution)/shard_map/concatenate | solution.py:87
  42.2 53.6 %all_to_all.10 = bf16[32,10,3456]{2,1,0:T(8,128)(2,1)S(1)} all-to-all(bf16[32,10,3456]{2,1,0:T(8,128)(2,1)} %concatenate.23), channel_id=1, replica_groups=mesh['expert'=32,'rep'=4] {'expert'}, dimensions={0} | all-to-all | bytes 4423680 | tf_op jit(solution)/shard_map/all_to_all | solution.py:88
  95.7 1.7 copy.34
  97.7 83.8 %all-gather.2.cloned.1.call-done = bf16[128,10,3456]{2,0,1:T(8,128)(2,1)} async-done(((bf16[32,10,3456]{2,0,1:T(8,128)(2,1)}), bf16[128,10,3456]{2,0,1:T(8,128)(2,1)}) %all-gather.2.cloned.1.call-update) | async-done | bytes 8847376 | tf_op jit(solution)/shard_map/all_gather | solution.py:89
  181.5 13.5 %copy.35 = bf16[128,10,3456]{2,1,0:T(8,128)(2,1)} copy(bf16[128,10,3456]{2,0,1:T(8,128)(2,1)} %all-gather.2.cloned.1.call-done) | data formatting | bytes 17694720 | tf_op jit(solution)/shard_map/all_gather | solution.py:89
  195.0 14.4 %reshape.80 = bf16[1280,3456]{1,0:T(8,128)(2,1)} reshape(bf16[128,10,3456]{2,1,0:T(8,128)(2,1)} %copy.35) | data formatting | bytes 17694720 | tf_op jit(solution)/shard_map/reshape | solution.py:90
  209.4 1.1 convert_reduce_fusion.1
  210.6 6.8 %fusion.7 = f32[1280,1024]{1,0:T(8,128)S(1)} fusion(bf16[1280,3456]{1,0:T(8,128)(2,1)} %reshape.80, bf16[1,1664,1024]{2,1,0:T(8,128)(2,1)S(1)} %copy-done), kind=kOutput, calls=%fused_computation.15 | convolution fusion | flops 4362076160 | bytes 12910592 | tf_op jit(solution)/shard_map/dot_general | solution.py:17
  217.5 11.1 %multiply_reduce_fusion = (f32[1280]{0:T(1024)S(1)}, bf16[1280,1024]{1,0:T(8,128)(2,1)}) fusion(f32[1280,1024]{1,0:T(8,128)S(1)} %fusion.7, f32[1280]{0:T(1024)S(1)} %convert_reduce_fusion.1, bf16[1,1024,1664]{2,1,0:T(8,128)(2,1)S(1)} %copy-done.8, bf16[1280,3456]{1,0:T(8,128)(2,1)} %reshape.80), kind=kOutput, calls=%fused_computation.10 | convolution fusion | flops 4380425216 | bytes 15542272 | tf_op jit(solution)/shard_map/dot_general | solution.py:17
  228.6 1.3 concatenate.31
  229.9 10.1 %fusion.12 = f32[4,320,1664]{2,1,0:T(8,128)} fusion(bf16[4,320,1024]{2,1,0:T(8,128)(2,1)} %bitcast.44, bf16[1,1664,1024]{2,1,0:T(8,128)(2,1)S(1)} %copy-done), kind=kOutput, calls=%fused_computation.20 | convolution fusion | flops 4362076160 | bytes 14548992 | tf_op jit(solution)/shard_map/dot_general | solution.py:17
  240.0 10.2 %concatenate.25 = f32[4,320,1792]{2,1,0:T(8,128)} concatenate(f32[4,320,1664]{2,1,0:T(8,128)} %fusion.12, f32[4,320,1]{2,1,0:T(8,128)} %concatenate.31, f32[4,320,127]{2,1,0:T(8,128)S(1)} %broadcast_in_dim.26), dimensions={2} | concatenate | bytes 18350080 | tf_op jit(solution)/shard_map/concatenate | solution.py:99
  250.3 88.1 %reduce-scatter.2.cloned.1.call-done = f32[1,320,1792]{2,1,0:T(8,128)} async-done(((f32[4,320,1792]{2,1,0:T(8,128)}), f32[1,320,1792]{2,1,0:T(8,128)}) %reduce-scatter.2.cloned.1.call-update) | async-done | bytes 2293776 | tf_op jit(solution)/shard_map/reduce_scatter | solution.py:104
  338.3 3.8 reshape.81
  342.2 7.8 %all-to-all-start.1 = ((f32[32,10,1792]{2,1,0:T(8,128)}), f32[32,10,1792]{2,1,0:T(8,128)}, u32[]{:S(2)}, u32[]{:S(2)}) async-start(f32[32,10,1792]{2,1,0:T(8,128)} %reshape.81), calls=%async_computation.2 | async-start | bytes 7340032 | tf_op jit(solution)/shard_map/all_to_all | solution.py:106
  350.3 8.8 %convolution_bitcast_fusion.1 = f32[1,1664,1024]{2,1,0:T(8,128)} fusion(bf16[1280,1024]{1,0:T(8,128)(2,1)S(1)} %copy-done.9, bf16[1280,3456]{1,0:T(8,128)(2,1)} %reshape.80), kind=kOutput, calls=%fused_computation.13 | convolution fusion | flops 4362076160 | bytes 13697024 | tf_op jit(solution)/shard_map/dot_general | solution.py:17
  359.1 10.2 %convolution_bitcast_fusion = f32[1,1024,1664]{2,1,0:T(8,128)} fusion(bf16[1280,3456]{1,0:T(8,128)(2,1)} %reshape.80, f32[1280]{0:T(1024)S(1)} %convert_reduce_fusion.1, f32[1280,1024]{1,0:T(8,128)} %copy-done.10), kind=kOutput, calls=%fused_computation.12 | convolution fusion | flops 4369940480 | bytes 16323584 | tf_op jit(solution)/shard_map/dot_general | solution.py:17
  369.4 26.3 %all-to-all-done.1 = f32[32,10,1792]{2,1,0:T(8,128)} async-done(((f32[32,10,1792]{2,1,0:T(8,128)}), f32[32,10,1792]{2,1,0:T(8,128)}, u32[]{:S(2)}, u32[]{:S(2)}) %all-to-all-start.1) | async-done | bytes 2293792 | tf_op jit(solution)/shard_map/all_to_all | solution.py:106
  395.7 4.6 reshape.82
  401.4 3.4 fusion.18
  405.0 1.3 fusion.48
  406.3 3.1 fusion.33
  410.2 2.6 fusion.32
  412.8 139.4 %all-reduce.2.cloned.1.call-done = f32[1664,34]{0,1:T(8,128)} async-done(((f32[1664,34]{0,1:T(8,128)}), f32[1664,34]{0,1:T(8,128)}) %all-reduce.2.cloned.1.call-update) | async-done | bytes 226320 | tf_op jit(solution)/shard_map/psum | solution.py:124
  552.2 1.5 slice_reduce_fusion.1
  553.7 1.6 slice.71
  (59 shorter events, 16.3 us)
Async XLA Ops:
  7.2 203.4 %copy-start = (bf16[1,1664,1024]{2,1,0:T(8,128)(2,1)S(1)}, bf16[1,1664,1024]{2,1,0:T(8,128)(2,1)}, u32[]{:S(2)}) copy-start(bf16[1,1664,1024]{2,1,0:T(8,128)(2,1)} %param.16) | copy-start | bytes 10223620
  7.2 174.4 %all-gather.2.cloned.1.call-start = ((), (), s32[]{:S(2)}) async-start(), calls=%async_computation.3 | async-start | bytes 11059200 | tf_op jit(solution)/shard_map/all_gather | solution.py:89
  13.4 0.8 copy-start.2
  97.5 240.8 %reduce-scatter.2.cloned.1.call-start = ((), (), s32[]{:S(2)}) async-start(), calls=%async_computation.4 | async-start | bytes 11468800 | tf_op jit(solution)/shard_map/reduce_scatter | solution.py:104
  210.6 6.9 %copy-start.8 = (bf16[1,1024,1664]{2,1,0:T(8,128)(2,1)S(1)}, bf16[1,1024,1664]{2,1,0:T(8,128)(2,1)}, u32[]{:S(2)}) copy-start(bf16[1,1024,1664]{2,1,0:T(8,128)(2,1)} %param.17) | copy-start | bytes 10223620
  217.5 11.1 %copy-start.10 = (f32[1280,1024]{1,0:T(8,128)}, f32[1280,1024]{1,0:T(8,128)S(1)}, u32[]{:S(2)}) copy-start(f32[1280,1024]{1,0:T(8,128)S(1)} %fusion.7) | copy-start | bytes 15728644
  250.2 100.0 %copy-start.4 = (s32[128,2]{0,1:T(2,128)S(1)}, s32[128,2]{0,1:T(2,128)}, u32[]{:S(2)}) copy-start(s32[128,2]{0,1:T(2,128)} %param.12) | copy-start | bytes 3076
  250.2 100.0 %copy-start.9 = (bf16[1280,1024]{1,0:T(8,128)(2,1)S(1)}, bf16[1280,1024]{1,0:T(8,128)(2,1)}, u32[]{:S(2)}) copy-start(bf16[1280,1024]{1,0:T(8,128)(2,1)} %get-tuple-element.19) | copy-start | bytes 7864324
  342.2 53.5 %all-to-all-start.1 = ((f32[32,10,1792]{2,1,0:T(8,128)}), f32[32,10,1792]{2,1,0:T(8,128)}, u32[]{:S(2)}, u32[]{:S(2)}) async-start(f32[32,10,1792]{2,1,0:T(8,128)} %reshape.81), calls=%async_computation.2 | async-start | bytes 7340032 | tf_op jit(solution)/shard_map/all_to_all | solution.py:106
  350.0 202.2 %all-reduce.2.cloned.1.call-start = ((), (), s32[]{:S(2)}) async-start(), calls=%async_computation.5 | async-start | bytes 532480 | tf_op jit(solution)/shard_map/psum | solution.py:124
  369.4 35.6 %copy-start.5 = (f32[128,1]{0,1:T(1,128)S(1)}, f32[128,1]{0,1:T(1,128)}, u32[]{:S(2)}) copy-start(f32[128,1]{0,1:T(1,128)} %get-tuple-element.15) | copy-start | bytes 1540
  369.4 35.6 %copy-start.6 = (f32[128,1]{0,1:T(1,128)S(1)}, f32[128,1]{0,1:T(1,128)}, u32[]{:S(2)}) copy-start(f32[128,1]{0,1:T(1,128)} %get-tuple-element.21) | copy-start | bytes 1540
  369.4 36.9 %copy-start.3 = (f32[1664]{0:T(1024)S(1)}, f32[1664]{0:T(1024)}, u32[]{:S(2)}) copy-start(f32[1664]{0:T(1024)} %param.13) | copy-start | bytes 19972
  369.4 40.8 %copy-start.7 = (pred[128]{0:T(512)(128)(4,1)S(1)}, pred[128]{0:T(512)(128)(4,1)}, u32[]{:S(2)}) copy-start(pred[128]{0:T(512)(128)(4,1)} %broadcast_in_dim.22) | copy-start | bytes 388
  395.7 159.7 %copy-start.1 = (bf16[1,1664,1024]{2,1,0:T(8,128)(2,1)S(1)}, bf16[1,1664,1024]{2,1,0:T(8,128)(2,1)}, u32[]{:S(2)}) copy-start(bf16[1,1664,1024]{2,1,0:T(8,128)(2,1)} %param.16) | copy-start | bytes 10223620
Sparse Core Ops, SparseCore 0:
  97.6 83.8 all-gather.1
  250.4 87.9 reduce-scatter.1
  410.3 141.8 all-reduce.1

commit v2 on v1

--- a/solution.py
+++ b/solution.py
@@ -53,6 +53,20 @@
     return (input_grad, gate_grad, grad_in, grad_out)
 
 
+def all_sum(part):
+    devices = lax.axis_size("expert") * lax.axis_size("rep")
+    flat = part.reshape(-1)
+    width = -(-flat.shape[0] // (devices * 128)) * 128
+    flat = jnp.pad(flat, (0, devices * width - flat.shape[0]))
+    pieces = lax.all_to_all(
+        flat.reshape(devices, width), ("expert", "rep"), split_axis=0, concat_axis=0, tiled=True
+    )
+    mine = jnp.sum(pieces, axis=0)
+    spread_out = jnp.broadcast_to(mine[None], (devices, width))
+    whole = lax.all_to_all(spread_out, ("expert", "rep"), split_axis=0, concat_axis=0, tiled=True)
+    return whole.reshape(-1)[: part.size].reshape(part.shape)
+
+
 def on_device(
     tokens, grad_grid, keep_order, expert_ids, norm_gain, norm_bias, router_weight, w_in, w_out
 ):
@@ -71,7 +85,7 @@
     expert_hits = jnp.sum(chosen, axis=1)
     before = jnp.cumsum(expert_hits, axis=0) - expert_hits
     slot_place = jnp.sum(before[:, None, :] * chosen, axis=2).astype(jnp.int32)
-    slot_index = expert_ids * capacity + slot_place
+    slot_index = slot_place * experts + expert_ids
     slot_ids = jnp.arange(experts * capacity, dtype=jnp.int32)
     spread = (slot_index[:, :, None] == slot_ids[None, None, :]).astype(jnp.float32)
     assign = jnp.sum(spread, axis=1)
@@ -84,9 +98,9 @@
     gate_block = jnp.concatenate(
         [send_gate[:, None], jnp.zeros((experts * capacity, lane - 1), jnp.bfloat16)], axis=1
     )
-    send = jnp.concatenate([send_rows, gate_block], axis=1).reshape(experts, capacity, -1)
-    got = lax.all_to_all(send, "expert", split_axis=0, concat_axis=0, tiled=True)
-    got = lax.all_gather(got, "rep", axis=0, tiled=True)
+    send = jnp.concatenate([send_rows, gate_block], axis=1).reshape(capacity, experts, -1)
+    got = lax.all_to_all(send, "expert", split_axis=1, concat_axis=1, tiled=True)
+    got = lax.all_gather(got, "rep", axis=0, tiled=False)
     got = got.reshape(-1, got.shape[-1])
     input_grad, gate_grad, grad_in, grad_out = expert_rows(
         got[:, :model_width],
@@ -102,8 +116,8 @@
     copies = lax.axis_size("rep")
     packed = packed.reshape(copies, slots_all // copies, -1)
     back = lax.psum_scatter(packed, "rep", scatter_dimension=0, tiled=True)
-    back = back.reshape(experts, capacity, -1)
-    ret = lax.all_to_all(back, "expert", split_axis=0, concat_axis=0, tiled=True)
+    back = back.reshape(capacity, experts, -1)
+    ret = lax.all_to_all(back, "expert", split_axis=1, concat_axis=1, tiled=True)
     ret = ret.reshape(experts * capacity, -1)
     ret_rows = ret[:, :model_width]
     ret_gate = ret[:, model_width]
@@ -121,9 +135,8 @@
     )
     local_gain = jnp.sum(normed_grad * normed, axis=0)
     local_bias = jnp.sum(normed_grad, axis=0)
-    summed = lax.psum(
-        jnp.concatenate([local_router, local_gain[:, None], local_bias[:, None]], axis=1),
-        ("expert", "rep"),
+    summed = all_sum(
+        jnp.concatenate([local_router, local_gain[:, None], local_bias[:, None]], axis=1)
     )
     grad_router = summed[:, :experts]
     grad_gain = summed[:, experts]

time: 564 us -> 434 us (0.77)
  waiting for transfers between devices: 338 us -> 216 us
  local copies, waits for them, and re-layouts: 71.1 us -> 49.3 us
  starting transfers between devices: 8.35 us -> 25.6 us
    psum x1 -> x0, waiting for transfers between devices: 139 us -> none  [on_device(): lax.psum(jnp.concatenate([local_router, local_gain[:, None], local_bias[:...]
    all_to_all x1 -> x3, waiting for transfers between devices: 26.3 us -> 43.9 us  [the longest x1 35.4 us: on_device(): lax.all_to_all(back, 'expert', split_axis=1, concat_axis=1, tiled=True)]
    all_to_all x1 -> x3, starting transfers between devices: 7.83 us -> 25.3 us  [the longest x1 10 us: all_sum(): lax.all_to_all(spread_out, ('expert', 'rep'), split_axis=0, concat_axis=0...]
    reshape x3, local copies, waits for them, and re-layouts: 22.8 us -> 8.46 us  [the longest x1 4.86 us: on_device(): back = back.reshape(capacity, experts, -1)]
    all_gather x1 -> x0, local copies, waits for them, and re-layouts: 13.5 us -> none  [on_device(): got = lax.all_gather(got, 'rep', axis=0, tiled=True)]
    concatenate x3 -> x4, local copies, waits for them, and re-layouts: 11.6 us -> 9.67 us  [on_device(): jnp.concatenate([send_rows, gate_block], axis=1)]
  transfers between devices with their start and end apart: 4 -> 5, of which waited for: 4 -> 5; matrix products, arithmetic and copies ran while one was open for 4% -> 5% of each run, Pallas kernels for 0% -> 0%
where the time goes in v2:
time: 434 us; the launch traced here: 433 us
  waiting for transfers between devices  216 us (50%)
  matrix products  56.6 us (13%)
  blocking collectives  53.6 us (12%)
  local copies, waits for them, and re-layouts  49.3 us (11%)
  starting transfers between devices  25.6 us (6%)
  other arithmetic  17.2 us (4%)
  between operations  14.4 us (3%)
    reduce_scatter x1, waiting for transfers between devices, on_device(): back = lax.psum_scatter(packed, 'rep', scatter_dimension=0, tiled=True)  88.1 us
    all_gather x1, waiting for transfers between devices, on_device(): got = lax.all_gather(got, 'rep', axis=0, tiled=False)  83.8 us
    all_to_all x1, blocking collectives, on_device(): lax.all_to_all(send, 'expert', split_axis=1, concat_axis=1, tiled=True)  53.6 us
    dot_general x6, matrix products, contract(): lax.dot_general(left, right, (((left_axis,), (right_axis,)), ((), ())), p...  50.7 us
    all_to_all x1, waiting for transfers between devices, on_device(): lax.all_to_all(back, 'expert', split_axis=1, concat_axis=1, tiled=True)  35.4 us
    concatenate x2, local copies, waits for them, and re-layouts, on_device(): jnp.concatenate([input_grad, gate_grad[:, None], jnp.zeros((slots_all, la...  11.6 us
    all_to_all x1, starting transfers between devices, all_sum(): lax.all_to_all(spread_out, ('expert', 'rep'), split_axis=0, concat_axis=0...  10 us
    concatenate x4, local copies, waits for them, and re-layouts, on_device(): jnp.concatenate([send_rows, gate_block], axis=1)  9.67 us
  transfers between devices with their start and end apart: 5, of which 5 were waited for; matrix products, arithmetic and copies ran while one was open for 5% of the time, Pallas kernels for 0%

profile of v2, /device:TPU:1, one launch (start us, length us, event | category | flops | bytes accessed | tf_op | source)
XLA Modules:
  0.0 432.6 jit_solution(6749543664415583424)
XLA Ops:
  10.6 1.3 fusion.34
  12.0 1.4 fusion.27
  14.1 1.5 fusion.55
  22.0 3.3 gather_fusion
  26.4 1.8 convolution_convert_fusion
  28.2 3.0 copy.59
  31.9 6.4 %concatenate.23 = bf16[10,32,3456]{2,0,1:T(8,128)(2,1)} concatenate(bf16[10,32,3328]{2,0,1:T(8,128)(2,1)} %copy.59, bf16[10,32,1]{2,0,1:T(8,128)(2,1)S(1)} %copy.60, bf16[10,32,127]{2,0,1:T(8,128)(2,1)} %broadcast_in_dim.27), dimensions={2} | concatenate | bytes 4423680 | tf_op jit(solution)/shard_map/concatenate | solution.py:101
  38.3 53.6 %all_to_all.25 = bf16[10,32,3456]{2,0,1:T(8,128)(2,1)S(1)} all-to-all(bf16[10,32,3456]{2,0,1:T(8,128)(2,1)} %concatenate.23), channel_id=1, replica_groups=mesh['expert'=32,'rep'=4] {'expert'}, dimensions={1} | all-to-all | bytes 4423680 | tf_op jit(solution)/shard_map/all_to_all | solution.py:102
  91.8 1.7 copy.61
  93.8 83.8 %all-gather.3.cloned.1.call-done = bf16[40,32,3456]{2,1,0:T(8,128)(2,1)} async-done(((bf16[10,32,3456]{2,1,0:T(8,128)(2,1)}), bf16[40,32,3456]{2,1,0:T(8,128)(2,1)}) %all-gather.3.cloned.1.call-update) | async-done | bytes 8847376 | tf_op jit(solution)/shard_map/all_gather | solution.py:103
  178.8 6.8 %fusion.7 = f32[1280,1024]{1,0:T(8,128)S(1)} fusion(bf16[1280,3456]{1,0:T(8,128)(2,1)} %bitcast.56, bf16[1,1664,1024]{2,1,0:T(8,128)(2,1)S(1)} %copy-done), kind=kOutput, calls=%fused_computation.15 | convolution fusion | flops 4362076160 | bytes 12910592 | tf_op jit(solution)/shard_map/dot_general | solution.py:17
  185.7 11.1 %multiply_reduce_fusion = (f32[1280]{0:T(1024)S(1)}, bf16[1280,1024]{1,0:T(8,128)(2,1)}) fusion(f32[1280,1024]{1,0:T(8,128)S(1)} %fusion.7, f32[1280]{0:T(1024)S(1)} %convert_reduce_fusion.1, bf16[1,1024,1664]{2,1,0:T(8,128)(2,1)S(1)} %copy-done.14, bf16[1280,3456]{1,0:T(8,128)(2,1)} %bitcast.57), kind=kOutput, calls=%fused_computation.10 | convolution fusion | flops 4380425216 | bytes 15542272 | tf_op jit(solution)/shard_map/dot_general | solution.py:17
  196.8 1.3 concatenate.30
  198.1 10.1 %fusion.12 = f32[4,320,1664]{2,1,0:T(8,128)} fusion(bf16[4,320,1024]{2,1,0:T(8,128)(2,1)} %bitcast.61, bf16[1,1664,1024]{2,1,0:T(8,128)(2,1)S(1)} %copy-done), kind=kOutput, calls=%fused_computation.20 | convolution fusion | flops 4362076160 | bytes 14548992 | tf_op jit(solution)/shard_map/dot_general | solution.py:17
  208.2 10.3 %concatenate.25 = f32[4,320,1792]{2,1,0:T(8,128)} concatenate(f32[4,320,1664]{2,1,0:T(8,128)} %fusion.12, f32[4,320,1]{2,1,0:T(8,128)} %concatenate.30, f32[4,320,127]{2,1,0:T(8,128)S(1)} %broadcast_in_dim.28), dimensions={2} | concatenate | bytes 18350080 | tf_op jit(solution)/shard_map/concatenate | solution.py:113
  218.5 88.1 %reduce-scatter.2.cloned.1.call-done = f32[1,320,1792]{2,1,0:T(8,128)} async-done(((f32[4,320,1792]{2,1,0:T(8,128)}), f32[1,320,1792]{2,1,0:T(8,128)}) %reduce-scatter.2.cloned.1.call-update) | async-done | bytes 2293776 | tf_op jit(solution)/shard_map/reduce_scatter | solution.py:118
  306.6 4.9 %copy.63 = f32[10,32,1792]{2,0,1:T(8,128)} copy(f32[10,32,1792]{2,1,0:T(8,128)} %bitcast.54) | data formatting | bytes 4587520 | tf_op jit(solution)/shard_map/reshape | solution.py:119
  311.4 7.8 %all-to-all-start.1 = ((f32[10,32,1792]{2,0,1:T(8,128)}), f32[10,32,1792]{2,0,1:T(8,128)}, u32[]{:S(2)}, u32[]{:S(2)}) async-start(f32[10,32,1792]{2,0,1:T(8,128)} %copy.63), calls=%async_computation.2 | async-start | bytes 7340032 | tf_op jit(solution)/shard_map/all_to_all | solution.py:120
  319.3 10.2 %convolution_bitcast_fusion = f32[1,1024,1664]{2,1,0:T(8,128)} fusion(bf16[1280,3456]{1,0:T(8,128)(2,1)} %bitcast.58, f32[1280]{0:T(1024)S(1)} %convert_reduce_fusion.1, f32[1280,1024]{1,0:T(8,128)} %copy-done.15), kind=kOutput, calls=%fused_computation.12 | convolution fusion | flops 4369940480 | bytes 16323584 | tf_op jit(solution)/shard_map/dot_general | solution.py:17
  329.6 35.4 %all-to-all-done.1 = f32[10,32,1792]{2,0,1:T(8,128)} async-done(((f32[10,32,1792]{2,0,1:T(8,128)}), f32[10,32,1792]{2,0,1:T(8,128)}, u32[]{:S(2)}, u32[]{:S(2)}) %all-to-all-start.1) | async-done | bytes 2293792 | tf_op jit(solution)/shard_map/all_to_all | solution.py:120
  365.0 3.4 copy.64
  368.5 1.7 fusion.18
  370.8 2.1 fusion.33
  374.7 7.5 %all-to-all-start.2 = ((f32[128,1,512]{2,1,0:T(1,128)}), f32[128,1,512]{2,1,0:T(1,128)}, u32[]{:S(2)}, u32[]{:S(2)}) async-start(f32[128,1,512]{2,1,0:T(1,128)} %bitcast.15), calls=%async_computation.3 | async-start | bytes 524288 | tf_op jit(solution)/shard_map/all_to_all | solution.py:61
  382.2 10.7 %convolution_bitcast_fusion.1 = f32[1,1664,1024]{2,1,0:T(8,128)} fusion(bf16[1280,1024]{1,0:T(8,128)(2,1)} %get-tuple-element.49, bf16[1280,3456]{1,0:T(8,128)(2,1)} %bitcast.59), kind=kOutput, calls=%fused_computation.13 | convolution fusion | flops 4362076160 | bytes 13697024 | tf_op jit(solution)/shard_map/dot_general | solution.py:17
  395.1 10.0 %all-to-all-start.3 = ((f32[128,1,512]{2,1,0:T(1,128)}), f32[128,1,512]{2,1,0:T(1,128)}, u32[]{:S(2)}, u32[]{:S(2)}) async-start(f32[128,1,512]{2,1,0:T(1,128)} %broadcast_in_dim.61), calls=%async_computation.4 | async-start | bytes 524288 | tf_op jit(solution)/shard_map/all_to_all | solution.py:66
  405.2 2.6 fusion.32
  407.8 8.3 %all-to-all-done.3 = f32[128,1,512]{2,1,0:T(1,128)} async-done(((f32[128,1,512]{2,1,0:T(1,128)}), f32[128,1,512]{2,1,0:T(1,128)}, u32[]{:S(2)}, u32[]{:S(2)}) %all-to-all-start.3) | async-done | bytes 262176 | tf_op jit(solution)/shard_map/all_to_all | solution.py:66
  416.1 1.6 slice.75
  417.7 2.9 reshape.105
  420.6 3.0 slice_reduce_fusion
  423.6 2.1 copy.67
  (76 shorter events, 18.6 us)
Async XLA Ops:
  7.2 171.6 %copy-start = (bf16[1,1664,1024]{2,1,0:T(8,128)(2,1)S(1)}, bf16[1,1664,1024]{2,1,0:T(8,128)(2,1)}, u32[]{:S(2)}) copy-start(bf16[1,1664,1024]{2,1,0:T(8,128)(2,1)} %param.16) | copy-start | bytes 10223620
  7.2 170.5 %all-gather.3.cloned.1.call-start = ((), (), s32[]{:S(2)}) async-start(), calls=%async_computation.6 | async-start | bytes 11059200 | tf_op jit(solution)/shard_map/all_gather | solution.py:103
  13.4 0.8 copy-start.3
  20.1 1.6 copy-start.9
  93.6 213.0 %reduce-scatter.2.cloned.1.call-start = ((), (), s32[]{:S(2)}) async-start(), calls=%async_computation.5 | async-start | bytes 11468800 | tf_op jit(solution)/shard_map/reduce_scatter | solution.py:118
  178.8 6.9 %copy-start.14 = (bf16[1,1024,1664]{2,1,0:T(8,128)(2,1)S(1)}, bf16[1,1024,1664]{2,1,0:T(8,128)(2,1)}, u32[]{:S(2)}) copy-start(bf16[1,1024,1664]{2,1,0:T(8,128)(2,1)} %param.17) | copy-start | bytes 10223620
  185.7 11.1 %copy-start.15 = (f32[1280,1024]{1,0:T(8,128)}, f32[1280,1024]{1,0:T(8,128)S(1)}, u32[]{:S(2)}) copy-start(f32[1280,1024]{1,0:T(8,128)S(1)} %fusion.7) | copy-start | bytes 15728644
  306.6 12.7 %copy-start.8 = (s32[128,2]{0,1:T(2,128)S(1)}, s32[128,2]{0,1:T(2,128)}, u32[]{:S(2)}) copy-start(s32[128,2]{0,1:T(2,128)} %param.12) | copy-start | bytes 3076
  311.4 53.5 %all-to-all-start.1 = ((f32[10,32,1792]{2,0,1:T(8,128)}), f32[10,32,1792]{2,0,1:T(8,128)}, u32[]{:S(2)}, u32[]{:S(2)}) async-start(f32[10,32,1792]{2,0,1:T(8,128)} %copy.63), calls=%async_computation.2 | async-start | bytes 7340032 | tf_op jit(solution)/shard_map/all_to_all | solution.py:120
  329.5 39.0 %copy-start.5 = (f32[128,320]{0,1:T(8,128)S(1)}, f32[128,320]{0,1:T(8,128)}, u32[]{:S(2)}) copy-start(f32[128,320]{0,1:T(8,128)} %convert_reduce_fusion.2) | copy-start | bytes 491524
  329.5 40.7 %copy-start.10 = (s32[128,2]{0,1:T(2,128)S(1)}, s32[128,2]{0,1:T(2,128)}, u32[]{:S(2)}) copy-start(s32[128,2]{0,1:T(2,128)} %copy-done.9) | copy-start | bytes 3076
  329.5 40.9 %copy-start.11 = (f32[128,1]{0,1:T(1,128)S(1)}, f32[128,1]{0,1:T(1,128)}, u32[]{:S(2)}) copy-start(f32[128,1]{0,1:T(1,128)} %get-tuple-element.45) | copy-start | bytes 1540
  329.5 40.9 %copy-start.12 = (f32[128,1]{0,1:T(1,128)S(1)}, f32[128,1]{0,1:T(1,128)}, u32[]{:S(2)}) copy-start(f32[128,1]{0,1:T(1,128)} %get-tuple-element.51) | copy-start | bytes 1540
  329.5 40.9 %copy-start.4 = (bf16[128,1664]{1,0:T(8,128)(2,1)S(1)}, bf16[128,1664]{1,0:T(8,128)(2,1)}, u32[]{:S(2)}) copy-start(bf16[128,1664]{1,0:T(8,128)(2,1)} %copy-done.3) | copy-start | bytes 1277956
  329.6 41.2 %copy-start.2 = (bf16[128,1664]{1,0:T(8,128)(2,1)S(1)}, bf16[128,1664]{1,0:T(8,128)(2,1)}, u32[]{:S(2)}) copy-start(bf16[128,1664]{1,0:T(8,128)(2,1)} %param.9) | copy-start | bytes 1277956
  329.6 41.2 %copy-start.7 = (f32[1664]{0:T(1024)S(1)}, f32[1664]{0:T(1024)}, u32[]{:S(2)}) copy-start(f32[1664]{0:T(1024)} %param.13) | copy-start | bytes 19972
  365.0 5.9 %copy-start.6 = (f32[1664,32]{0,1:T(8,128)S(1)}, f32[1664,32]{0,1:T(8,128)}, u32[]{:S(2)}) copy-start(f32[1664,32]{0,1:T(8,128)} %param.15) | copy-start | bytes 638980
  374.7 18.4 %all-to-all-start.2 = ((f32[128,1,512]{2,1,0:T(1,128)}), f32[128,1,512]{2,1,0:T(1,128)}, u32[]{:S(2)}, u32[]{:S(2)}) async-start(f32[128,1,512]{2,1,0:T(1,128)} %bitcast.15), calls=%async_computation.3 | async-start | bytes 524288 | tf_op jit(solution)/shard_map/all_to_all | solution.py:61
  382.2 23.0 %copy-start.13 = (pred[128]{0:T(512)(128)(4,1)S(1)}, pred[128]{0:T(512)(128)(4,1)}, u32[]{:S(2)}) copy-start(pred[128]{0:T(512)(128)(4,1)} %broadcast_in_dim.24) | copy-start | bytes 388
  382.2 43.5 %copy-start.1 = (bf16[1,1664,1024]{2,1,0:T(8,128)(2,1)S(1)}, bf16[1,1664,1024]{2,1,0:T(8,128)(2,1)}, u32[]{:S(2)}) copy-start(bf16[1,1664,1024]{2,1,0:T(8,128)(2,1)} %param.16) | copy-start | bytes 10223620
  395.1 21.0 %all-to-all-start.3 = ((f32[128,1,512]{2,1,0:T(1,128)}), f32[128,1,512]{2,1,0:T(1,128)}, u32[]{:S(2)}, u32[]{:S(2)}) async-start(f32[128,1,512]{2,1,0:T(1,128)} %broadcast_in_dim.61), calls=%async_computation.4 | async-start | bytes 524288 | tf_op jit(solution)/shard_map/all_to_all | solution.py:66
Sparse Core Ops, SparseCore 0:
  93.7 83.8 all-gather.2
  218.6 87.9 reduce-scatter.1

commit v3 on v2

--- a/solution.py
+++ b/solution.py
@@ -110,17 +110,27 @@
         w_out[0],
     )
     slots_all = input_grad.shape[0]
-    packed = jnp.concatenate(
-        [input_grad, gate_grad[:, None], jnp.zeros((slots_all, lane - 1), jnp.float32)], axis=1
+    rep_at = lax.axis_index("rep")
+    gate_hi = gate_grad.astype(jnp.bfloat16)
+    gate_lo = (gate_grad - gate_hi.astype(jnp.float32)).astype(jnp.bfloat16)
+    cols = jnp.arange(lane, dtype=jnp.int32)[None, :]
+    zero = jnp.zeros((), jnp.bfloat16)
+    gate_cols = jnp.where(
+        cols == 2 * rep_at,
+        gate_hi[:, None],
+        jnp.where(cols == 2 * rep_at + 1, gate_lo[:, None], zero),
     )
+    packed = jnp.concatenate([input_grad.astype(jnp.bfloat16), gate_cols], axis=1)
     copies = lax.axis_size("rep")
     packed = packed.reshape(copies, slots_all // copies, -1)
     back = lax.psum_scatter(packed, "rep", scatter_dimension=0, tiled=True)
     back = back.reshape(capacity, experts, -1)
     ret = lax.all_to_all(back, "expert", split_axis=1, concat_axis=1, tiled=True)
     ret = ret.reshape(experts * capacity, -1)
-    ret_rows = ret[:, :model_width]
-    ret_gate = ret[:, model_width]
+    ret_rows = ret[:, :model_width].astype(jnp.float32)
+    ret_gate = jnp.sum(
+        ret[:, model_width : model_width + 2 * copies].astype(jnp.float32), axis=1
+    )
     grad_w_in = grad_in[None]
     grad_w_out = grad_out[None]
     mixed_grad = jnp.dot(assign, ret_rows, precision=PRECISE)

time: 434 us -> 359 us (0.83)
  waiting for transfers between devices: 216 us -> 159 us
  local copies, waits for them, and re-layouts: 49.3 us -> 40.6 us
  starting transfers between devices: 25.6 us -> 17.9 us
  matrix products: 56.6 us -> 50.2 us
  other arithmetic: 17.2 us -> 22 us
    reduce_scatter x1, waiting for transfers between devices: 88.1 us -> 40.6 us  [on_device(): back = lax.psum_scatter(packed, 'rep', scatter_dimension=0, tiled=True)]
    all_to_all x1, waiting for transfers between devices: 35.4 us -> 15 us  [on_device(): lax.all_to_all(back, 'expert', split_axis=1, concat_axis=1, tiled=True)]
    concatenate x2 -> x0, local copies, waits for them, and re-layouts: 11.6 us -> none  [on_device(): jnp.concatenate([input_grad, gate_grad[:, None], jnp.zeros((slots_all, la...]
    all_to_all x1, waiting for transfers between devices: 0.22 us -> 11.1 us  [all_sum(): lax.all_to_all(flat.reshape(devices, width), ('expert', 'rep'), split_axi...]
    dot_general x6, matrix products: 50.7 us -> 45.2 us  [contract(): lax.dot_general(left, right, (((left_axis,), (right_axis,)), ((), ())), p...]
    all_to_all x1, starting transfers between devices: 10 us -> 4.69 us  [all_sum(): lax.all_to_all(spread_out, ('expert', 'rep'), split_axis=0, concat_axis=0...]
  transfers between devices with their start and end apart: 5 -> 5, of which waited for: 5 -> 5; matrix products, arithmetic and copies ran while one was open for 5% -> 6% of each run, Pallas kernels for 0% -> 0%
where the time goes in v3:
time: 359 us; the launch traced here: 358 us
  waiting for transfers between devices  159 us (44%)
  blocking collectives  53.6 us (15%)
  matrix products  50.2 us (14%)
  local copies, waits for them, and re-layouts  40.6 us (11%)
  other arithmetic  22 us (6%)
  starting transfers between devices  17.9 us (5%)
  between operations  14.4 us (4%)
    all_gather x1, waiting for transfers between devices, on_device(): got = lax.all_gather(got, 'rep', axis=0, tiled=False)  83.8 us
    all_to_all x1, blocking collectives, on_device(): lax.all_to_all(send, 'expert', split_axis=1, concat_axis=1, tiled=True)  53.6 us
    dot_general x6, matrix products, contract(): lax.dot_general(left, right, (((left_axis,), (right_axis,)), ((), ())), p...  45.2 us
    reduce_scatter x1, waiting for transfers between devices, on_device(): back = lax.psum_scatter(packed, 'rep', scatter_dimension=0, tiled=True)  40.6 us
    all_to_all x1, waiting for transfers between devices, on_device(): lax.all_to_all(back, 'expert', split_axis=1, concat_axis=1, tiled=True)  15 us
    all_to_all x1, waiting for transfers between devices, all_sum(): lax.all_to_all(flat.reshape(devices, width), ('expert', 'rep'), split_axi...  11.1 us
    concatenate x4, local copies, waits for them, and re-layouts, on_device(): jnp.concatenate([send_rows, gate_block], axis=1)  9.68 us
    all_to_all x1, waiting for transfers between devices, all_sum(): lax.all_to_all(spread_out, ('expert', 'rep'), split_axis=0, concat_axis=0...  8.47 us
  transfers between devices with their start and end apart: 5, of which 5 were waited for; matrix products, arithmetic and copies ran while one was open for 6% of the time, Pallas kernels for 0%

profile of v3, /device:TPU:1, one launch (start us, length us, event | category | flops | bytes accessed | tf_op | source)
XLA Modules:
  0.0 357.6 jit_solution(4836806173632230478)
XLA Ops:
  7.2 1.4 bitcast_or_fusion
  14.4 1.5 fusion.54
  24.2 3.3 gather_fusion
  28.7 1.8 convolution_convert_fusion.1
  30.5 3.0 copy.62
  34.1 6.4 %concatenate.20 = bf16[10,32,3456]{2,0,1:T(8,128)(2,1)} concatenate(bf16[10,32,3328]{2,0,1:T(8,128)(2,1)} %copy.62, bf16[10,32,1]{2,0,1:T(8,128)(2,1)S(1)} %copy.63, bf16[10,32,127]{2,0,1:T(8,128)(2,1)} %broadcast_in_dim.90), dimensions={2} | concatenate | bytes 4423680 | tf_op jit(solution)/shard_map/concatenate | solution.py:101
  40.5 53.6 %all_to_all.25 = bf16[10,32,3456]{2,0,1:T(8,128)(2,1)S(1)} all-to-all(bf16[10,32,3456]{2,0,1:T(8,128)(2,1)} %concatenate.20), channel_id=1, replica_groups=mesh['expert'=32,'rep'=4] {'expert'}, dimensions={1} | all-to-all | bytes 4423680 | tf_op jit(solution)/shard_map/all_to_all | solution.py:102
  94.1 1.7 copy.64
  96.1 83.8 %all-gather.3.cloned.1.call-done = bf16[40,32,3456]{2,1,0:T(8,128)(2,1)} async-done(((bf16[10,32,3456]{2,1,0:T(8,128)(2,1)}), bf16[40,32,3456]{2,1,0:T(8,128)(2,1)}) %all-gather.3.cloned.1.call-update) | async-done | bytes 8847376 | tf_op jit(solution)/shard_map/all_gather | solution.py:103
  181.2 8.3 %fusion.10 = f32[1280,1024]{0,1:T(8,128)S(1)} fusion(bf16[1280,3456]{1,0:T(8,128)(2,1)} %bitcast.57, bf16[1,1024,1664]{2,1,0:T(8,128)(2,1)} %param.17), kind=kOutput, calls=%fused_computation.20 | convolution fusion | flops 4362076160 | bytes 12910592 | tf_op jit(solution)/shard_map/dot_general | solution.py:17
  189.6 10.4 %fusion.5 = (bf16[1280,1024]{0,1:T(8,128)(2,1)S(1)}, f32[1280]{0:T(1024)S(1)}, f32[1280,1024]{0,1:T(8,128)}) fusion(f32[1280,1024]{0,1:T(8,128)S(1)} %fusion.10, f32[1280]{0:T(1024)S(1)} %convert_reduce_fusion.1, bf16[1,1664,1024]{2,1,0:T(8,128)(2,1)S(1)} %copy-done, bf16[1280,3456]{1,0:T(8,128)(2,1)S(1)} %bitcast.62), kind=kOutput, calls=%fused_computation.9 | convolution fusion | flops 4380425216 | bytes 20788224 | tf_op jit(solution)/shard_map/dot_general | solution.py:17
  200.0 5.3 %convolution_convert_fusion = bf16[1280,1664]{1,0:T(8,128)(2,1)S(1)} fusion(bf16[1280,1024]{0,1:T(8,128)(2,1)S(1)} %get-tuple-element.56, bf16[1,1664,1024]{2,1,0:T(8,128)(2,1)S(1)} %copy-done), kind=kOutput, calls=%fused_computation.2 | convolution fusion | flops 4364206080 | bytes 10289152 | tf_op jit(solution)/shard_map/dot_general | solution.py:17
  205.7 2.5 pad_maximum_fusion
  209.9 8.9 %convolution_bitcast_fusion.1 = f32[1,1664,1024]{2,1,0:T(8,128)} fusion(bf16[1280,1024]{0,1:T(8,128)(2,1)S(1)} %copy-done.13, bf16[1280,3456]{1,0:T(8,128)(2,1)} %bitcast.58), kind=kOutput, calls=%fused_computation.15 | convolution fusion | flops 4362076160 | bytes 13697024 | tf_op jit(solution)/shard_map/dot_general | solution.py:17
  218.8 40.6 %reduce-scatter.2.cloned.1.call-done = bf16[1,320,1792]{2,1,0:T(8,128)(2,1)} async-done(((bf16[4,320,1792]{2,1,0:T(8,128)(2,1)}), bf16[1,320,1792]{2,1,0:T(8,128)(2,1)}) %reduce-scatter.2.cloned.1.call-update) | async-done | bytes 1146896 | tf_op jit(solution)/shard_map/reduce_scatter | solution.py:126
  259.4 3.1 copy.65
  262.5 7.8 %all-to-all-start.1 = ((bf16[10,32,1792]{2,0,1:T(8,128)(2,1)}), bf16[10,32,1792]{2,0,1:T(8,128)(2,1)S(1)}, u32[]{:S(2)}, u32[]{:S(2)}) async-start(bf16[10,32,1792]{2,0,1:T(8,128)(2,1)} %copy.65), calls=%async_computation.2 | async-start | bytes 3670016 | tf_op jit(solution)/shard_map/all_to_all | solution.py:128
  270.3 10.5 %convolution_bitcast_fusion = f32[1,1024,1664]{2,1,0:T(8,128)} fusion(bf16[1280,3456]{1,0:T(8,128)(2,1)} %bitcast.59, f32[1280]{0:T(1024)S(1)} %convert_reduce_fusion.1, f32[1280,1024]{0,1:T(8,128)} %get-tuple-element.60), kind=kOutput, calls=%fused_computation.14 | convolution fusion | flops 4369940480 | bytes 16323584 | tf_op jit(solution)/shard_map/dot_general | solution.py:17
  280.9 15.0 %all-to-all-done.1 = bf16[10,32,1792]{2,0,1:T(8,128)(2,1)S(1)} async-done(((bf16[10,32,1792]{2,0,1:T(8,128)(2,1)}), bf16[10,32,1792]{2,0,1:T(8,128)(2,1)S(1)}, u32[]{:S(2)}, u32[]{:S(2)}) %all-to-all-start.1) | async-done | bytes 1146912 | tf_op jit(solution)/shard_map/all_to_all | solution.py:128
  297.8 2.0 fusion.32
  300.5 2.3 copy.67
  302.9 2.6 reshape.119
  305.4 1.6 pad.4
  307.1 5.2 %all-to-all-start.2 = ((f32[128,1,512]{2,1,0:T(1,128)}), f32[128,1,512]{2,1,0:T(1,128)}, u32[]{:S(2)}, u32[]{:S(2)}) async-start(f32[128,1,512]{2,1,0:T(1,128)} %bitcast.55), calls=%async_computation.3 | async-start | bytes 524288 | tf_op jit(solution)/shard_map/all_to_all | solution.py:61
  312.3 11.1 %all-to-all-done.2 = f32[128,1,512]{2,1,0:T(1,128)} async-done(((f32[128,1,512]{2,1,0:T(1,128)}), f32[128,1,512]{2,1,0:T(1,128)}, u32[]{:S(2)}, u32[]{:S(2)}) %all-to-all-start.2) | async-done | bytes 262176 | tf_op jit(solution)/shard_map/all_to_all | solution.py:61
  325.4 4.7 %all-to-all-start.3 = ((f32[128,1,512]{2,1,0:T(1,128)}), f32[128,1,512]{2,1,0:T(1,128)}, u32[]{:S(2)}, u32[]{:S(2)}) async-start(f32[128,1,512]{2,1,0:T(1,128)} %broadcast_in_dim.100), calls=%async_computation.4 | async-start | bytes 524288 | tf_op jit(solution)/shard_map/all_to_all | solution.py:66
  330.1 2.6 fusion.31
  332.7 8.5 %all-to-all-done.3 = f32[128,1,512]{2,1,0:T(1,128)} async-done(((f32[128,1,512]{2,1,0:T(1,128)}), f32[128,1,512]{2,1,0:T(1,128)}, u32[]{:S(2)}, u32[]{:S(2)}) %all-to-all-start.3) | async-done | bytes 262176 | tf_op jit(solution)/shard_map/all_to_all | solution.py:66
  341.2 1.7 slice.75
  342.8 2.9 reshape.121
  345.7 3.0 slice_reduce_fusion
  348.7 2.1 copy.69
  (81 shorter events, 24.2 us)
Async XLA Ops:
  7.2 182.4 %copy-start = (bf16[1,1664,1024]{2,1,0:T(8,128)(2,1)S(1)}, bf16[1,1664,1024]{2,1,0:T(8,128)(2,1)}, u32[]{:S(2)}) copy-start(bf16[1,1664,1024]{2,1,0:T(8,128)(2,1)} %param.16) | copy-start | bytes 10223620
  7.2 172.7 %all-gather.3.cloned.1.call-start = ((), (), s32[]{:S(2)}) async-start(), calls=%async_computation.6 | async-start | bytes 11059200 | tf_op jit(solution)/shard_map/all_gather | solution.py:103
  13.6 0.8 copy-start.3
  95.8 163.6 %reduce-scatter.2.cloned.1.call-start = ((), (), s32[]{:S(2)}) async-start(), calls=%async_computation.5 | async-start | bytes 5734400 | tf_op jit(solution)/shard_map/reduce_scatter | solution.py:126
  179.9 9.7 %slice-start = ((s8[8847360]{0:T(1024)(128)(4,1)}), s8[4194304]{0:T(1024)(128)(4,1)S(1)}, s32[]{:S(2)}) async-start(s8[8847360]{0:T(1024)(128)(4,1)} %bitcast.60), calls=%async_computation.7 | async-start | bytes 8388608
  181.2 8.4 %slice-start.1 = ((s8[8847360]{0:T(1024)(128)(4,1)}), s8[4194304]{0:T(1024)(128)(4,1)S(1)}, s32[]{:S(2)}) async-start(s8[8847360]{0:T(1024)(128)(4,1)} %bitcast.60), calls=%async_computation.8 | async-start | bytes 8388608
  181.2 8.4 %slice-start.2 = ((s8[8847360]{0:T(1024)(128)(4,1)}), s8[458752]{0:T(1024)(128)(4,1)S(1)}, s32[]{:S(2)}) async-start(s8[8847360]{0:T(1024)(128)(4,1)} %bitcast.60), calls=%async_computation.9 | async-start | bytes 917504
  200.0 5.3 %copy-start.12 = (bf16[1280,1024]{0,1:T(8,128)(2,1)}, bf16[1280,1024]{0,1:T(8,128)(2,1)S(1)}, u32[]{:S(2)}) copy-start(bf16[1280,1024]{0,1:T(8,128)(2,1)S(1)} %get-tuple-element.56) | copy-start | bytes 7864324
  208.1 0.7 copy-start.8
  208.1 1.8 copy-start.13
  262.5 33.3 %all-to-all-start.1 = ((bf16[10,32,1792]{2,0,1:T(8,128)(2,1)}), bf16[10,32,1792]{2,0,1:T(8,128)(2,1)S(1)}, u32[]{:S(2)}, u32[]{:S(2)}) async-start(bf16[10,32,1792]{2,0,1:T(8,128)(2,1)} %copy.65), calls=%async_computation.2 | async-start | bytes 3670016 | tf_op jit(solution)/shard_map/all_to_all | solution.py:128
  270.3 26.0 %copy-start.5 = (f32[128,320]{0,1:T(8,128)S(1)}, f32[128,320]{0,1:T(8,128)}, u32[]{:S(2)}) copy-start(f32[128,320]{0,1:T(8,128)} %convert_reduce_fusion.2) | copy-start | bytes 491524
  280.8 16.6 %copy-start.9 = (f32[128,1]{0,1:T(1,128)S(1)}, f32[128,1]{0,1:T(1,128)}, u32[]{:S(2)}) copy-start(f32[128,1]{0,1:T(1,128)} %get-tuple-element.53) | copy-start | bytes 1540
  280.8 16.6 %copy-start.10 = (f32[128,1]{0,1:T(1,128)S(1)}, f32[128,1]{0,1:T(1,128)}, u32[]{:S(2)}) copy-start(f32[128,1]{0,1:T(1,128)} %get-tuple-element.59) | copy-start | bytes 1540
  280.8 16.6 %copy-start.4 = (bf16[128,1664]{1,0:T(8,128)(2,1)S(1)}, bf16[128,1664]{1,0:T(8,128)(2,1)}, u32[]{:S(2)}) copy-start(bf16[128,1664]{1,0:T(8,128)(2,1)} %copy-done.3) | copy-start | bytes 1277956
  280.8 16.9 %copy-start.2 = (bf16[128,1664]{1,0:T(8,128)(2,1)S(1)}, bf16[128,1664]{1,0:T(8,128)(2,1)}, u32[]{:S(2)}) copy-start(bf16[128,1664]{1,0:T(8,128)(2,1)} %param.9) | copy-start | bytes 1277956
  280.9 16.9 %copy-start.6 = (f32[1664,32]{0,1:T(8,128)S(1)}, f32[1664,32]{0,1:T(8,128)}, u32[]{:S(2)}) copy-start(f32[1664,32]{0,1:T(8,128)} %param.15) | copy-start | bytes 638980
  280.9 16.9 %copy-start.7 = (f32[1664]{0:T(1024)S(1)}, f32[1664]{0:T(1024)}, u32[]{:S(2)}) copy-start(f32[1664]{0:T(1024)} %param.13) | copy-start | bytes 19972
  296.3 33.8 %copy-start.11 = (pred[128]{0:T(512)(128)(4,1)S(1)}, pred[128]{0:T(512)(128)(4,1)}, u32[]{:S(2)}) copy-start(pred[128]{0:T(512)(128)(4,1)} %broadcast_in_dim.58) | copy-start | bytes 388
  300.5 50.2 %copy-start.1 = (bf16[1,1664,1024]{2,1,0:T(8,128)(2,1)S(1)}, bf16[1,1664,1024]{2,1,0:T(8,128)(2,1)}, u32[]{:S(2)}) copy-start(bf16[1,1664,1024]{2,1,0:T(8,128)(2,1)} %param.16) | copy-start | bytes 10223620
  307.1 16.3 %all-to-all-start.2 = ((f32[128,1,512]{2,1,0:T(1,128)}), f32[128,1,512]{2,1,0:T(1,128)}, u32[]{:S(2)}, u32[]{:S(2)}) async-start(f32[128,1,512]{2,1,0:T(1,128)} %bitcast.55), calls=%async_computation.3 | async-start | bytes 524288 | tf_op jit(solution)/shard_map/all_to_all | solution.py:61
  325.4 15.8 %all-to-all-start.3 = ((f32[128,1,512]{2,1,0:T(1,128)}), f32[128,1,512]{2,1,0:T(1,128)}, u32[]{:S(2)}, u32[]{:S(2)}) async-start(f32[128,1,512]{2,1,0:T(1,128)} %broadcast_in_dim.100), calls=%async_computation.4 | async-start | bytes 524288 | tf_op jit(solution)/shard_map/all_to_all | solution.py:66
Sparse Core Ops, SparseCore 0:
  95.9 83.8 all-gather.2
  208.3 51.0 reduce-scatter.1

commit v4 on v3

--- a/solution.py
+++ b/solution.py
@@ -99,38 +99,48 @@
         [send_gate[:, None], jnp.zeros((experts * capacity, lane - 1), jnp.bfloat16)], axis=1
     )
     send = jnp.concatenate([send_rows, gate_block], axis=1).reshape(capacity, experts, -1)
-    got = lax.all_to_all(send, "expert", split_axis=1, concat_axis=1, tiled=True)
-    got = lax.all_gather(got, "rep", axis=0, tiled=False)
-    got = got.reshape(-1, got.shape[-1])
-    input_grad, gate_grad, grad_in, grad_out = expert_rows(
-        got[:, :model_width],
-        got[:, model_width : 2 * model_width],
-        got[:, 2 * model_width],
-        w_in[0],
-        w_out[0],
-    )
-    slots_all = input_grad.shape[0]
     rep_at = lax.axis_index("rep")
-    gate_hi = gate_grad.astype(jnp.bfloat16)
-    gate_lo = (gate_grad - gate_hi.astype(jnp.float32)).astype(jnp.bfloat16)
+    copies = lax.axis_size("rep")
     cols = jnp.arange(lane, dtype=jnp.int32)[None, :]
     zero = jnp.zeros((), jnp.bfloat16)
-    gate_cols = jnp.where(
-        cols == 2 * rep_at,
-        gate_hi[:, None],
-        jnp.where(cols == 2 * rep_at + 1, gate_lo[:, None], zero),
-    )
-    packed = jnp.concatenate([input_grad.astype(jnp.bfloat16), gate_cols], axis=1)
-    copies = lax.axis_size("rep")
-    packed = packed.reshape(copies, slots_all // copies, -1)
-    back = lax.psum_scatter(packed, "rep", scatter_dimension=0, tiled=True)
-    back = back.reshape(capacity, experts, -1)
-    ret = lax.all_to_all(back, "expert", split_axis=1, concat_axis=1, tiled=True)
-    ret = ret.reshape(experts * capacity, -1)
+    half = capacity // 2
+    bounds = ((0, half), (half, capacity))
+    ret_parts, in_parts, out_parts = ([], [], [])
+    for low, high in bounds:
+        got = lax.all_to_all(send[low:high], "expert", split_axis=1, concat_axis=1, tiled=True)
+        got = lax.all_gather(got, "rep", axis=0, tiled=False)
+        got = got.reshape(-1, got.shape[-1])
+        input_grad, gate_grad, grad_in, grad_out = expert_rows(
+            got[:, :model_width],
+            got[:, model_width : 2 * model_width],
+            got[:, 2 * model_width],
+            w_in[0],
+            w_out[0],
+        )
+        in_parts.append(grad_in)
+        out_parts.append(grad_out)
+        rows_here = input_grad.shape[0]
+        gate_hi = gate_grad.astype(jnp.bfloat16)
+        gate_lo = (gate_grad - gate_hi.astype(jnp.float32)).astype(jnp.bfloat16)
+        gate_cols = jnp.where(
+            cols == 2 * rep_at,
+            gate_hi[:, None],
+            jnp.where(cols == 2 * rep_at + 1, gate_lo[:, None], zero),
+        )
+        packed = jnp.concatenate([input_grad.astype(jnp.bfloat16), gate_cols], axis=1)
+        packed = packed.reshape(copies, rows_here // copies, -1)
+        back = lax.psum_scatter(packed, "rep", scatter_dimension=0, tiled=True)
+        back = back.reshape(high - low, experts, -1)
+        ret_parts.append(
+            lax.all_to_all(back, "expert", split_axis=1, concat_axis=1, tiled=True)
+        )
+    ret = jnp.concatenate(ret_parts, axis=0).reshape(experts * capacity, -1)
     ret_rows = ret[:, :model_width].astype(jnp.float32)
     ret_gate = jnp.sum(
         ret[:, model_width : model_width + 2 * copies].astype(jnp.float32), axis=1
     )
+    grad_in = in_parts[0] + in_parts[1]
+    grad_out = out_parts[0] + out_parts[1]
     grad_w_in = grad_in[None]
     grad_w_out = grad_out[None]
     mixed_grad = jnp.dot(assign, ret_rows, precision=PRECISE)

time: 359 us -> 342 us (0.953)
  waiting for transfers between devices: 159 us -> 113 us
  matrix products: 50.2 us -> 68.4 us
  blocking collectives: 53.6 us -> 62.6 us
  starting transfers between devices: 17.9 us -> 25 us
  local copies, waits for them, and re-layouts: 40.6 us -> 36.1 us
    all_gather x1 -> x2, waiting for transfers between devices: 83.8 us -> 61 us  [on_device(): got = lax.all_gather(got, 'rep', axis=0, tiled=False)]
    dot_general x6 -> x11, matrix products: 45.2 us -> 63.3 us  [contract(): lax.dot_general(left, right, (((left_axis,), (right_axis,)), ((), ())), p...]
    reduce_scatter x1 -> x2, waiting for transfers between devices: 40.6 us -> 24.3 us  [on_device(): back = lax.psum_scatter(packed, 'rep', scatter_dimension=0, tiled=True)]
    all_to_all x1 -> x2, blocking collectives: 53.6 us -> 62.6 us  [on_device(): lax.all_to_all(send[low:high], 'expert', split_axis=1, concat_axis=1, til...]
    all_to_all x1 -> x2, starting transfers between devices: 7.78 us -> 15.5 us  [on_device(): lax.all_to_all(back, 'expert', split_axis=1, concat_axis=1, tiled=True)]
    all_to_all x1 -> x2, waiting for transfers between devices: 15 us -> 7.93 us  [on_device(): lax.all_to_all(back, 'expert', split_axis=1, concat_axis=1, tiled=True)]
    concatenate x4 -> x1, local copies, waits for them, and re-layouts: 9.68 us -> 4.55 us  [on_device(): jnp.concatenate([send_rows, gate_block], axis=1)]
    slice x0 -> x3, local copies, waits for them, and re-layouts: none -> 4.78 us  [on_device(): send[low:high]]
  transfers between devices with their start and end apart: 5 -> 8, of which waited for: 5 -> 7; matrix products, arithmetic and copies ran while one was open for 6% -> 16% of each run, Pallas kernels for 0% -> 0%
where the time goes in v4:
time: 342 us; the launch traced here: 341 us
  waiting for transfers between devices  113 us (33%)
  matrix products  68.4 us (20%)
  blocking collectives  62.6 us (18%)
  local copies, waits for them, and re-layouts  36.1 us (11%)
  starting transfers between devices  25 us (7%)
  other arithmetic  21.5 us (6%)
  between operations  14.2 us (4%)
    dot_general x11, matrix products, contract(): lax.dot_general(left, right, (((left_axis,), (right_axis,)), ((), ())), p...  63.3 us
    all_to_all x2, blocking collectives, on_device(): lax.all_to_all(send[low:high], 'expert', split_axis=1, concat_axis=1, til...  62.6 us
    all_gather x2, waiting for transfers between devices, on_device(): got = lax.all_gather(got, 'rep', axis=0, tiled=False)  61 us
    reduce_scatter x2, waiting for transfers between devices, on_device(): back = lax.psum_scatter(packed, 'rep', scatter_dimension=0, tiled=True)  24.3 us
    all_to_all x2, starting transfers between devices, on_device(): lax.all_to_all(back, 'expert', split_axis=1, concat_axis=1, tiled=True)  15.5 us
    all_to_all x1, waiting for transfers between devices, all_sum(): lax.all_to_all(flat.reshape(devices, width), ('expert', 'rep'), split_axi...  11.3 us
    all_to_all x1, waiting for transfers between devices, all_sum(): lax.all_to_all(spread_out, ('expert', 'rep'), split_axis=0, concat_axis=0...  8.31 us
    all_to_all x2, waiting for transfers between devices, on_device(): lax.all_to_all(back, 'expert', split_axis=1, concat_axis=1, tiled=True)  7.93 us
  transfers between devices with their start and end apart: 8, of which 7 were waited for; matrix products, arithmetic and copies ran while one was open for 16% of the time, Pallas kernels for 0%

profile of v4, /device:TPU:1, one launch (start us, length us, event | category | flops | bytes accessed | tf_op | source)
XLA Modules:
  0.0 340.7 jit_solution(12944417093301560041)
XLA Ops:
  22.8 3.3 gather_fusion
  27.3 3.1 convolution_convert_fusion
  30.5 4.5 %concatenate.19 = bf16[320,3456]{1,0:T(8,128)(2,1)} concatenate(bf16[320,3328]{1,0:T(8,128)(2,1)} %convolution_convert_fusion, bf16[320,1]{1,0:T(8,128)(2,1)} %broadcast_in_dim.126, bf16[320,127]{1,0:T(8,128)(2,1)S(1)} %broadcast_in_dim.113), dimensions={1} | concatenate | bytes 4423680 | tf_op jit(solution)/shard_map/concatenate | solution.py:101
  35.0 2.7 fusion.81
  38.1 34.2 %all_to_all.35 = bf16[5,32,3456]{2,0,1:T(8,128)(2,1)S(1)} all-to-all(bf16[5,32,3456]{2,0,1:T(8,128)(2,1)S(1)} %copy.74), channel_id=1, replica_groups=mesh['expert'=32,'rep'=4] {'expert'}, dimensions={1} | all-to-all | bytes 2211840 | tf_op jit(solution)/shard_map/all_to_all | solution.py:110
  75.2 28.4 %all_to_all.36 = bf16[5,32,3456]{2,0,1:T(8,128)(2,1)S(1)} all-to-all(bf16[5,32,3456]{2,0,1:T(8,128)(2,1)S(1)} %copy.77), channel_id=1, replica_groups=mesh['expert'=32,'rep'=4] {'expert'}, dimensions={1} | all-to-all | bytes 2211840 | tf_op jit(solution)/shard_map/all_to_all | solution.py:110
  104.9 16.0 %all-gather.5.cloned.1.call-done = bf16[20,32,3456]{2,1,0:T(8,128)(2,1)} async-done(((bf16[5,32,3456]{2,1,0:T(8,128)(2,1)}), bf16[20,32,3456]{2,1,0:T(8,128)(2,1)}) %all-gather.5.cloned.1.call-update) | async-done | bytes 4423696 | tf_op jit(solution)/shard_map/all_gather | solution.py:111
  121.9 6.7 %fusion.10 = f32[640,1024]{1,0:T(8,128)} fusion(bf16[1,1024,1664]{2,1,0:T(8,128)(2,1)} %param.17, bf16[640,3456]{1,0:T(8,128)(2,1)} %bitcast.84), kind=kOutput, calls=%fused_computation.16 | convolution fusion | flops 2181038080 | bytes 8159232 | tf_op jit(solution)/shard_map/dot_general | solution.py:17
  128.6 45.0 %all-gather.7.cloned.1.call-done = bf16[20,32,3456]{2,1,0:T(8,128)(2,1)} async-done(((bf16[5,32,3456]{2,1,0:T(8,128)(2,1)}), bf16[20,32,3456]{2,1,0:T(8,128)(2,1)}) %all-gather.7.cloned.1.call-update) | async-done | bytes 4423696 | tf_op jit(solution)/shard_map/all_gather | solution.py:111
  174.7 5.3 %fusion.8 = f32[640,1024]{1,0:T(8,128)S(1)} fusion(bf16[1,1024,1664]{2,1,0:T(8,128)(2,1)} %param.17, bf16[640,3456]{1,0:T(8,128)(2,1)} %bitcast.77), kind=kOutput, calls=%fused_computation.14 | convolution fusion | flops 2181038080 | bytes 8159232 | tf_op jit(solution)/shard_map/dot_general | solution.py:17
  180.1 4.9 %fusion.23 = (bf16[640,1024]{1,0:T(8,128)(2,1)S(1)}, f32[640]{0:T(1024)S(1)}, f32[640,1024]{1,0:T(8,128)}) fusion(f32[640,1024]{1,0:T(8,128)S(1)} %copy-done.16, f32[640]{0:T(1024)S(1)} %convert_reduce_fusion.2, bf16[1,1664,1024]{2,1,0:T(8,128)(2,1)S(1)} %copy-done, bf16[640,3456]{1,0:T(8,128)(2,1)S(1)} %bitcast.87), kind=kOutput, calls=%fused_computation.25 | convolution fusion | flops 2190212608 | bytes 12098048 | tf_op jit(solution)/shard_map/dot_general | solution.py:17
  184.9 2.6 fusion.12
  187.5 5.3 %fusion.29 = (bf16[640,1024]{1,0:T(8,128)(2,1)}, f32[640]{0:T(1024)S(1)}, f32[640,1024]{1,0:T(8,128)}) fusion(f32[640,1024]{1,0:T(8,128)S(1)} %fusion.8, f32[640]{0:T(1024)S(1)} %convert_reduce_fusion.1, bf16[1,1664,1024]{2,1,0:T(8,128)(2,1)S(1)} %copy-done, bf16[640,3456]{1,0:T(8,128)(2,1)S(1)} %bitcast.82), kind=kOutput, calls=%fused_computation.31 | convolution fusion | flops 2190212608 | bytes 12098048 | tf_op jit(solution)/shard_map/dot_general | solution.py:17
  195.8 3.9 %fusion.15 = bf16[640,1664]{1,0:T(8,128)(2,1)S(1)} fusion(bf16[640,1024]{1,0:T(8,128)(2,1)} %get-tuple-element.60, bf16[1,1664,1024]{2,1,0:T(8,128)(2,1)S(1)} %copy-done), kind=kOutput, calls=%fused_computation.19 | convolution fusion | flops 2182103040 | bytes 6848512 | tf_op jit(solution)/shard_map/dot_general | solution.py:17
  202.4 6.8 %fusion.37 = f32[1024,1664]{1,0:T(8,128)} fusion(bf16[640,3456]{1,0:T(8,128)(2,1)} %bitcast.85, f32[640]{0:T(1024)S(1)} %convert_reduce_fusion.2, f32[640,1024]{1,0:T(8,128)S(1)} %copy-done.12), kind=kOutput, calls=%fused_computation.48 | convolution fusion | flops 2184970240 | bytes 11569664 | tf_op jit(solution)/shard_map/dot_general | solution.py:17
  209.1 18.4 %reduce-scatter.3.cloned.1.call-done = bf16[1,160,1792]{2,1,0:T(8,128)(2,1)} async-done(((bf16[4,160,1792]{2,1,0:T(8,128)(2,1)}), bf16[1,160,1792]{2,1,0:T(8,128)(2,1)}) %reduce-scatter.3.cloned.1.call-update) | async-done | bytes 573456 | tf_op jit(solution)/shard_map/reduce_scatter | solution.py:132
  227.5 2.3 copy.76
  229.8 7.8 %all-to-all-start.1 = ((bf16[5,32,1792]{2,0,1:T(8,128)(2,1)}), bf16[5,32,1792]{2,0,1:T(8,128)(2,1)S(1)}, u32[]{:S(2)}, u32[]{:S(2)}) async-start(bf16[5,32,1792]{2,0,1:T(8,128)(2,1)} %copy.76), calls=%async_computation.2 | async-start | bytes 1835008 | tf_op jit(solution)/shard_map/all_to_all | solution.py:135
  237.6 10.9 %add_bitcast_fusion = f32[1,1024,1664]{2,1,0:T(8,128)} fusion(f32[1024,1664]{1,0:T(8,128)} %fusion.37, bf16[640,3456]{1,0:T(8,128)(2,1)} %bitcast.78, f32[640]{0:T(1024)S(1)} %convert_reduce_fusion.1, f32[640,1024]{1,0:T(8,128)} %get-tuple-element.69), kind=kOutput, calls=%fused_computation.1 | convolution fusion | flops 2186674176 | bytes 18385408 | tf_op jit(solution)/shard_map/dot_general | solution.py:17
  248.5 6.4 %fusion.34 = f32[1664,1024]{1,0:T(8,128)} fusion(bf16[640,1024]{1,0:T(8,128)(2,1)S(1)} %copy-done.15, bf16[640,3456]{1,0:T(8,128)(2,1)} %bitcast.86), kind=kOutput, calls=%fused_computation.45 | convolution fusion | flops 2181038080 | bytes 10256384 | tf_op jit(solution)/shard_map/dot_general | solution.py:17
  254.9 5.9 %reduce-scatter.5.cloned.1.call-done = bf16[1,160,1792]{2,1,0:T(8,128)(2,1)} async-done(((bf16[4,160,1792]{2,1,0:T(8,128)(2,1)}), bf16[1,160,1792]{2,1,0:T(8,128)(2,1)}) %reduce-scatter.5.cloned.1.call-update) | async-done | bytes 573456 | tf_op jit(solution)/shard_map/reduce_scatter | solution.py:132
  260.8 2.3 copy.79
  263.2 7.8 %all-to-all-start.3 = ((bf16[5,32,1792]{2,0,1:T(8,128)(2,1)}), bf16[5,32,1792]{2,0,1:T(8,128)(2,1)S(1)}, u32[]{:S(2)}, u32[]{:S(2)}) async-start(bf16[5,32,1792]{2,0,1:T(8,128)(2,1)} %copy.79), calls=%async_computation.5 | async-start | bytes 1835008 | tf_op jit(solution)/shard_map/all_to_all | solution.py:135
  270.9 7.5 %add_bitcast_fusion.1 = f32[1,1664,1024]{2,1,0:T(8,128)} fusion(f32[1664,1024]{1,0:T(8,128)} %fusion.34, bf16[640,1024]{1,0:T(8,128)(2,1)S(1)} %copy-done.13, bf16[640,3456]{1,0:T(8,128)(2,1)} %bitcast.79), kind=kOutput, calls=%fused_computation.2 | convolution fusion | flops 2182742016 | bytes 17072128 | tf_op jit(solution)/shard_map/dot_general | solution.py:17
  278.5 7.9 %all-to-all-done.3 = bf16[5,32,1792]{2,0,1:T(8,128)(2,1)S(1)} async-done(((bf16[5,32,1792]{2,0,1:T(8,128)(2,1)}), bf16[5,32,1792]{2,0,1:T(8,128)(2,1)S(1)}, u32[]{:S(2)}, u32[]{:S(2)}) %all-to-all-start.3) | async-done | bytes 573472 | tf_op jit(solution)/shard_map/all_to_all | solution.py:135
  292.2 4.2 %all-to-all-start.4 = ((f32[128,1,512]{2,1,0:T(1,128)}), f32[128,1,512]{2,1,0:T(1,128)S(1)}, u32[]{:S(2)}, u32[]{:S(2)}) async-start(f32[128,1,512]{2,1,0:T(1,128)} %bitcast.18), calls=%async_computation.6 | async-start | bytes 524288 | tf_op jit(solution)/shard_map/all_to_all | solution.py:61
  296.4 11.3 %all-to-all-done.4 = f32[128,1,512]{2,1,0:T(1,128)S(1)} async-done(((f32[128,1,512]{2,1,0:T(1,128)}), f32[128,1,512]{2,1,0:T(1,128)S(1)}, u32[]{:S(2)}, u32[]{:S(2)}) %all-to-all-start.4) | async-done | bytes 262176 | tf_op jit(solution)/shard_map/all_to_all | solution.py:61
  308.7 4.7 %all-to-all-start.5 = ((f32[128,1,512]{2,1,0:T(1,128)}), f32[128,1,512]{2,1,0:T(1,128)}, u32[]{:S(2)}, u32[]{:S(2)}) async-start(f32[128,1,512]{2,1,0:T(1,128)} %broadcast_in_dim.125), calls=%async_computation.7 | async-start | bytes 524288 | tf_op jit(solution)/shard_map/all_to_all | solution.py:66
  313.4 2.8 fusion.58
  316.2 8.3 %all-to-all-done.5 = f32[128,1,512]{2,1,0:T(1,128)} async-done(((f32[128,1,512]{2,1,0:T(1,128)}), f32[128,1,512]{2,1,0:T(1,128)}, u32[]{:S(2)}, u32[]{:S(2)}) %all-to-all-start.5) | async-done | bytes 262176 | tf_op jit(solution)/shard_map/all_to_all | solution.py:66
  326.2 2.9 reshape.139
  329.0 3.0 slice_reduce_fusion
  (106 shorter events, 39.5 us)
Async XLA Ops:
  7.2 172.9 %copy-start = (bf16[1,1664,1024]{2,1,0:T(8,128)(2,1)S(1)}, bf16[1,1664,1024]{2,1,0:T(8,128)(2,1)}, u32[]{:S(2)}) copy-start(bf16[1,1664,1024]{2,1,0:T(8,128)(2,1)} %param.16) | copy-start | bytes 10223620
  7.2 11.8 %copy-start.9 = (s32[128,2]{0,1:T(2,128)S(1)}, s32[128,2]{0,1:T(2,128)}, u32[]{:S(2)}) copy-start(s32[128,2]{0,1:T(2,128)} %param.12) | copy-start | bytes 3076
  7.2 113.7 %all-gather.5.cloned.1.call-start = ((), (), s32[]{:S(2)}) async-start(), calls=%async_computation.10 | async-start | bytes 5529600 | tf_op jit(solution)/shard_map/all_gather | solution.py:111
  13.6 0.8 copy-start.3
  73.5 100.1 %all-gather.7.cloned.1.call-start = ((), (), s32[]{:S(2)}) async-start(), calls=%async_computation.11 | async-start | bytes 5529600 | tf_op jit(solution)/shard_map/all_gather | solution.py:111
  104.6 122.8 %reduce-scatter.3.cloned.1.call-start = ((), (), s32[]{:S(2)}) async-start(), calls=%async_computation.8 | async-start | bytes 2867200 | tf_op jit(solution)/shard_map/reduce_scatter | solution.py:132
  174.7 5.4 %copy-start.10 = (bf16[20,32,3456]{2,1,0:T(8,128)(2,1)S(1)}, bf16[20,32,3456]{2,1,0:T(8,128)(2,1)}, u32[]{:S(2)}) copy-start(bf16[20,32,3456]{2,1,0:T(8,128)(2,1)} %all-gather.5.cloned.1.call-done) | copy-start | bytes 13271044
  174.7 5.4 %copy-start.16 = (f32[640,1024]{1,0:T(8,128)S(1)}, f32[640,1024]{1,0:T(8,128)}, u32[]{:S(2)}) copy-start(f32[640,1024]{1,0:T(8,128)} %fusion.10) | copy-start | bytes 7864324
  174.7 12.8 %slice-start = ((s8[4423680]{0:T(1024)(128)(4,1)}), s8[4194304]{0:T(1024)(128)(4,1)S(1)}, s32[]{:S(2)}) async-start(s8[4423680]{0:T(1024)(128)(4,1)} %bitcast.80), calls=%async_computation.12 | async-start | bytes 8388608
  180.0 7.5 %slice-start.1 = ((s8[4423680]{0:T(1024)(128)(4,1)}), s8[229376]{0:T(1024)(128)(4,1)S(1)}, s32[]{:S(2)}) async-start(s8[4423680]{0:T(1024)(128)(4,1)} %bitcast.80), calls=%async_computation.13 | async-start | bytes 458752
  184.9 2.6 copy-start.14
  195.6 65.3 %reduce-scatter.5.cloned.1.call-start = ((), (), s32[]{:S(2)}) async-start(), calls=%async_computation.9 | async-start | bytes 2867200 | tf_op jit(solution)/shard_map/reduce_scatter | solution.py:132
  195.8 3.9 %copy-start.7 = (bf16[640,128]{1,0:T(8,128)(2,1)S(1)}, bf16[640,128]{1,0:T(8,128)(2,1)}, u32[]{:S(2)}) copy-start(bf16[640,128]{1,0:T(8,128)(2,1)} %get-tuple-element.65) | copy-start | bytes 491524
  199.8 2.6 copy-start.12
  229.8 33.4 %all-to-all-start.1 = ((bf16[5,32,1792]{2,0,1:T(8,128)(2,1)}), bf16[5,32,1792]{2,0,1:T(8,128)(2,1)S(1)}, u32[]{:S(2)}, u32[]{:S(2)}) async-start(bf16[5,32,1792]{2,0,1:T(8,128)(2,1)} %copy.76), calls=%async_computation.2 | async-start | bytes 1835008 | tf_op jit(solution)/shard_map/all_to_all | solution.py:135
  237.5 10.9 %copy-start.15 = (bf16[640,1024]{1,0:T(8,128)(2,1)S(1)}, bf16[640,1024]{1,0:T(8,128)(2,1)}, u32[]{:S(2)}) copy-start(bf16[640,1024]{1,0:T(8,128)(2,1)} %copy-done.14) | copy-start | bytes 3932164
  254.9 16.0 %copy-start.13 = (bf16[640,1024]{1,0:T(8,128)(2,1)S(1)}, bf16[640,1024]{1,0:T(8,128)(2,1)}, u32[]{:S(2)}) copy-start(bf16[640,1024]{1,0:T(8,128)(2,1)} %get-tuple-element.60) | copy-start | bytes 3932164
  263.2 23.3 %all-to-all-start.3 = ((bf16[5,32,1792]{2,0,1:T(8,128)(2,1)}), bf16[5,32,1792]{2,0,1:T(8,128)(2,1)S(1)}, u32[]{:S(2)}, u32[]{:S(2)}) async-start(bf16[5,32,1792]{2,0,1:T(8,128)(2,1)} %copy.79), calls=%async_computation.5 | async-start | bytes 1835008 | tf_op jit(solution)/shard_map/all_to_all | solution.py:135
  278.4 8.4 %copy-start.5 = (f32[128,320]{0,1:T(8,128)S(1)}, f32[128,320]{0,1:T(8,128)}, u32[]{:S(2)}) copy-start(f32[128,320]{0,1:T(8,128)} %convert_reduce_fusion.3) | copy-start | bytes 491524
  286.6 1.4 copy-start.11
  286.6 1.4 copy-start.4
  286.6 1.7 copy-start.2
  286.6 1.7 copy-start.6
  286.6 1.7 copy-start.8
  292.2 15.5 %all-to-all-start.4 = ((f32[128,1,512]{2,1,0:T(1,128)}), f32[128,1,512]{2,1,0:T(1,128)S(1)}, u32[]{:S(2)}, u32[]{:S(2)}) async-start(f32[128,1,512]{2,1,0:T(1,128)} %bitcast.18), calls=%async_computation.6 | async-start | bytes 524288 | tf_op jit(solution)/shard_map/all_to_all | solution.py:61
  308.7 15.8 %all-to-all-start.5 = ((f32[128,1,512]{2,1,0:T(1,128)}), f32[128,1,512]{2,1,0:T(1,128)}, u32[]{:S(2)}, u32[]{:S(2)}) async-start(f32[128,1,512]{2,1,0:T(1,128)} %broadcast_in_dim.125), calls=%async_computation.7 | async-start | bytes 524288 | tf_op jit(solution)/shard_map/all_to_all | solution.py:66
  313.4 20.7 %copy-start.1 = (bf16[1,1664,1024]{2,1,0:T(8,128)(2,1)S(1)}, bf16[1,1664,1024]{2,1,0:T(8,128)(2,1)}, u32[]{:S(2)}) copy-start(bf16[1,1664,1024]{2,1,0:T(8,128)(2,1)} %param.16) | copy-start | bytes 10223620
Sparse Core Ops, SparseCore 0:
  73.6 47.2 all-gather.4
  123.1 50.4 all-gather.6
  195.7 31.7 reduce-scatter.2
  229.8 31.0 reduce-scatter.4

commit v5 on v4

--- a/solution.py
+++ b/solution.py
@@ -67,7 +67,7 @@
     return whole.reshape(-1)[: part.size].reshape(part.shape)
 
 
-def on_device(
+def layer_body(
     tokens, grad_grid, keep_order, expert_ids, norm_gain, norm_bias, router_weight, w_in, w_out
 ):
     experts = router_weight.shape[1]
@@ -103,37 +103,46 @@
     copies = lax.axis_size("rep")
     cols = jnp.arange(lane, dtype=jnp.int32)[None, :]
     zero = jnp.zeros((), jnp.bfloat16)
+    is_hi = cols == 2 * rep_at
+    is_lo = cols == 2 * rep_at + 1
     half = capacity // 2
     bounds = ((0, half), (half, capacity))
     ret_parts, in_parts, out_parts = ([], [], [])
-    for low, high in bounds:
-        got = lax.all_to_all(send[low:high], "expert", split_axis=1, concat_axis=1, tiled=True)
-        got = lax.all_gather(got, "rep", axis=0, tiled=False)
+    for chunk, (low, high) in enumerate(bounds):
+        if chunk == 0:
+            got = lax.all_to_all(send[low:high], "expert", split_axis=1, concat_axis=1, tiled=True)
+            got = lax.all_gather(got, "rep", axis=0, tiled=False)
+        else:
+            part = send[low:high]
+            wide = jnp.broadcast_to(
+                part[:, :, None], (high - low, experts, copies, part.shape[-1])
+            ).reshape(high - low, experts * copies, -1)
+            got = lax.all_to_all(wide, ("expert", "rep"), split_axis=1, concat_axis=1, tiled=True)
+            got = got.reshape(high - low, experts, copies, -1).transpose(2, 0, 1, 3)
         got = got.reshape(-1, got.shape[-1])
+        weight_in, weight_out, at_hi, at_lo = (w_in[0], w_out[0], is_hi, is_lo)
+        if chunk:
+            weight_in, weight_out, at_hi, at_lo = lax.optimization_barrier(
+                (weight_in, weight_out, at_hi, at_lo)
+            )
         input_grad, gate_grad, grad_in, grad_out = expert_rows(
             got[:, :model_width],
             got[:, model_width : 2 * model_width],
             got[:, 2 * model_width],
-            w_in[0],
-            w_out[0],
+            weight_in,
+            weight_out,
         )
         in_parts.append(grad_in)
         out_parts.append(grad_out)
         rows_here = input_grad.shape[0]
         gate_hi = gate_grad.astype(jnp.bfloat16)
         gate_lo = (gate_grad - gate_hi.astype(jnp.float32)).astype(jnp.bfloat16)
-        gate_cols = jnp.where(
-            cols == 2 * rep_at,
-            gate_hi[:, None],
-            jnp.where(cols == 2 * rep_at + 1, gate_lo[:, None], zero),
-        )
+        gate_cols = jnp.where(at_hi, gate_hi[:, None], jnp.where(at_lo, gate_lo[:, None], zero))
         packed = jnp.concatenate([input_grad.astype(jnp.bfloat16), gate_cols], axis=1)
         packed = packed.reshape(copies, rows_here // copies, -1)
         back = lax.psum_scatter(packed, "rep", scatter_dimension=0, tiled=True)
         back = back.reshape(high - low, experts, -1)
-        ret_parts.append(
-            lax.all_to_all(back, "expert", split_axis=1, concat_axis=1, tiled=True)
-        )
+        ret_parts.append(lax.all_to_all(back, "expert", split_axis=1, concat_axis=1, tiled=True))
     ret = jnp.concatenate(ret_parts, axis=0).reshape(experts * capacity, -1)
     ret_rows = ret[:, :model_width].astype(jnp.float32)
     ret_gate = jnp.sum(
@@ -184,7 +193,7 @@
         P("expert", "rep", None),
     )
     return jax.shard_map(
-        on_device,
+        layer_body,
         mesh=mesh,
         in_specs=placed,
         out_specs=(

time: 342 us -> 380 us (1.11); the launches traced: 341 us -> 374 us
  blocking collectives: 62.6 us -> 0 us
  waiting for transfers between devices: 113 us -> 169 us
  local copies, waits for them, and re-layouts: 36.1 us -> 58.7 us
  starting transfers between devices: 25 us -> 42.2 us
    all_to_all x2 -> x4, waiting for transfers between devices: 7.93 us -> 142 us  [the longest x1 117 us: layer_body(): lax.all_to_all(wide, ('expert', 'rep'), split_axis=1, concat_axis=1, tile...]
    all_to_all x2 -> x0, blocking collectives: 62.6 us -> none  [on_device(): lax.all_to_all(send[low:high], 'expert', split_axis=1, concat_axis=1, til...]
    all_gather x2 -> x1, waiting for transfers between devices: 61 us -> 0.02 us  [layer_body(): got = lax.all_gather(got, 'rep', axis=0, tiled=False)]
    reduce_scatter x2, waiting for transfers between devices: 24.3 us -> 7.56 us  [layer_body(): back = lax.psum_scatter(packed, 'rep', scatter_dimension=0, tiled=True)]
    all_to_all x2 -> x4, starting transfers between devices: 15.5 us -> 31.8 us  [the longest x2 16 us: layer_body(): lax.all_to_all(back, 'expert', split_axis=1, concat_axis=1, tiled=True)]
    broadcast_in_dim x5 -> x7, local copies, waits for them, and re-layouts: 1.5 us -> 9.24 us  [the longest x2 7.74 us: layer_body(): jnp.broadcast_to(part[:, :, None], (high - low, experts, copies, part.sha...]
    reshape x2 -> x3, local copies, waits for them, and re-layouts: 4.62 us -> 9.48 us  [the longest x1 4.83 us: layer_body(): got = got.reshape(high - low, experts, copies, -1).transpose(2, 0, 1, 3)]
    slice x4 -> x3, local copies, waits for them, and re-layouts: 7.76 us -> 7.32 us  [the longest x2 4.33 us: layer_body(): send[low:high]]
  transfers between devices with their start and end apart: 8 -> 9, of which waited for: 7 -> 7; matrix products, arithmetic and copies ran while one was open for 16% -> 22% of each run, Pallas kernels for 0% -> 0%
where the time goes in v5:
time: 380 us; the launch traced here: 374 us
  waiting for transfers between devices  169 us (44%)
  matrix products  66.5 us (18%)
  local copies, waits for them, and re-layouts  58.7 us (15%)
  starting transfers between devices  42.2 us (11%)
  other arithmetic  22.5 us (6%)
  between operations  14.4 us (4%)
    all_to_all x1, waiting for transfers between devices, layer_body(): lax.all_to_all(wide, ('expert', 'rep'), split_axis=1, concat_axis=1, tile...  117 us
    dot_general x11, matrix products, contract(): lax.dot_general(left, right, (((left_axis,), (right_axis,)), ((), ())), p...  61.4 us
    all_to_all x1, waiting for transfers between devices, layer_body(): lax.all_to_all(send[low:high], 'expert', split_axis=1, concat_axis=1, til...  22 us
    all_to_all x2, starting transfers between devices, layer_body(): lax.all_to_all(back, 'expert', split_axis=1, concat_axis=1, tiled=True)  16 us
    all_to_all x1, waiting for transfers between devices, all_sum(): lax.all_to_all(flat.reshape(devices, width), ('expert', 'rep'), split_axi...  10.9 us
    all_to_all x1, starting transfers between devices, layer_body(): lax.all_to_all(send[low:high], 'expert', split_axis=1, concat_axis=1, til...  9.63 us
    all_to_all x1, waiting for transfers between devices, all_sum(): lax.all_to_all(spread_out, ('expert', 'rep'), split_axis=0, concat_axis=0...  8.48 us
    broadcast_in_dim x2, local copies, waits for them, and re-layouts, layer_body(): jnp.broadcast_to(part[:, :, None], (high - low, experts, copies, part.sha...  7.74 us
  transfers between devices with their start and end apart: 9, of which 7 were waited for; matrix products, arithmetic and copies ran while one was open for 22% of the time, Pallas kernels for 0%

profile of v5, /device:TPU:1, one launch (start us, length us, event | category | flops | bytes accessed | tf_op | source)
XLA Modules:
  0.0 373.6 jit_solution(2875890571761422750)
XLA Ops:
  22.8 3.3 gather_fusion
  27.2 3.1 convolution_convert_fusion
  30.4 4.5 %concatenate.19 = bf16[320,3456]{1,0:T(8,128)(2,1)} concatenate(bf16[320,3328]{1,0:T(8,128)(2,1)} %convolution_convert_fusion, bf16[320,1]{1,0:T(8,128)(2,1)} %broadcast_in_dim.148, bf16[320,127]{1,0:T(8,128)(2,1)S(1)} %broadcast_in_dim.129), dimensions={1} | concatenate | bytes 4423680 | tf_op jit(solution)/shard_map/concatenate | solution.py:101
  34.9 2.7 fusion.70
  39.2 9.6 %all-to-all-start = ((bf16[5,32,3456]{2,0,1:T(8,128)(2,1)}), bf16[5,32,3456]{2,0,1:T(8,128)(2,1)}, u32[]{:S(2)}, u32[]{:S(2)}) async-start(bf16[5,32,3456]{2,0,1:T(8,128)(2,1)} %copy.77), calls=%async_computation | async-start | bytes 3538944 | tf_op jit(solution)/shard_map/all_to_all | solution.py:113
  48.9 2.9 copy.80
  51.7 22.0 %all-to-all-done = bf16[5,32,3456]{2,0,1:T(8,128)(2,1)} async-done(((bf16[5,32,3456]{2,0,1:T(8,128)(2,1)}), bf16[5,32,3456]{2,0,1:T(8,128)(2,1)}, u32[]{:S(2)}, u32[]{:S(2)}) %all-to-all-start) | async-done | bytes 1105952 | tf_op jit(solution)/shard_map/all_to_all | solution.py:113
  73.8 4.9 %broadcast_in_dim.136 = bf16[5,32,4,3456]{3,0,2,1:T(8,128)(2,1)} broadcast(bf16[5,32,3456]{2,0,1:T(8,128)(2,1)} %copy.80), dimensions={0,1,3} | broadcast | bytes 5529600 | tf_op jit(solution)/shard_map/broadcast_in_dim | solution.py:117
  78.7 6.1 %all-to-all-start.2 = ((bf16[5,128,3456]{2,0,1:T(8,128)(2,1)}), bf16[5,128,3456]{2,0,1:T(8,128)(2,1)}, u32[]{:S(2)}, u32[]{:S(2)}) async-start(bf16[5,128,3456]{2,0,1:T(8,128)(2,1)} %bitcast.67), calls=%async_computation.3 | async-start | bytes 14155776 | tf_op jit(solution)/shard_map/all_to_all | solution.py:120
  84.8 2.6 copy.78
  88.0 116.6 %all-to-all-done.2 = bf16[5,128,3456]{2,0,1:T(8,128)(2,1)} async-done(((bf16[5,128,3456]{2,0,1:T(8,128)(2,1)}), bf16[5,128,3456]{2,0,1:T(8,128)(2,1)}, u32[]{:S(2)}, u32[]{:S(2)}) %all-to-all-start.2) | async-done | bytes 4423712 | tf_op jit(solution)/shard_map/all_to_all | solution.py:120
  204.6 4.8 %copy.96 = bf16[5,32,4,3456]{3,2,1,0:T(4,128)(2,1)S(1)} copy(bf16[5,32,4,3456]{3,0,2,1:T(8,128)(2,1)} %bitcast.10) | data formatting | bytes 8847360 | tf_op jit(solution)/shard_map/reshape | solution.py:121
  210.1 2.6 copy-done.11
  215.3 4.9 %fusion.11 = (bf16[640,1024]{1,0:T(8,128)(2,1)S(1)}, f32[640]{0:T(1024)S(1)}, f32[640,1024]{1,0:T(8,128)}) fusion(f32[640,1024]{1,0:T(8,128)S(1)} %fusion.16, f32[640]{0:T(1024)S(1)} %convert_reduce_fusion.1, bf16[1664,1024]{1,0:T(8,128)(2,1)S(1)} %bitcast.66, bf16[640,3456]{1,0:T(8,128)(2,1)S(1)} %bitcast.74), kind=kOutput, calls=%fused_computation.20 | convolution fusion | flops 2190212608 | bytes 12098048 | tf_op jit(solution)/shard_map/dot_general | solution.py:17
  226.0 5.4 %fusion.24 = f32[640,1024]{1,0:T(8,128)S(1)} fusion(bf16[640,3456]{1,0:T(8,128)(2,1)} %bitcast.85, bf16[1,1024,1664]{2,1,0:T(8,128)(2,1)} %param.17), kind=kOutput, calls=%fused_computation.42 | convolution fusion | flops 2181038080 | bytes 8159232 | tf_op jit(solution)/shard_map/dot_general | solution.py:17
  231.3 4.9 %fusion.5 = (bf16[640,1024]{1,0:T(8,128)(2,1)S(1)}, f32[640]{0:T(1024)S(1)}, f32[640,1024]{1,0:T(8,128)}) fusion(f32[640,1024]{1,0:T(8,128)S(1)} %fusion.24, f32[640]{0:T(1024)S(1)} %convert_reduce_fusion.2, bf16[1,1664,1024]{2,1,0:T(8,128)(2,1)S(1)} %copy-done, bf16[640,3456]{1,0:T(8,128)(2,1)S(1)} %bitcast.88), kind=kOutput, calls=%fused_computation.14 | convolution fusion | flops 2190212608 | bytes 12098048 | tf_op jit(solution)/shard_map/dot_general | solution.py:17
  236.5 2.6 convolution_convert_fusion.2
  240.7 8.5 %fusion.22 = f32[1024,1664]{1,0:T(8,128)} fusion(bf16[640,3456]{1,0:T(8,128)(2,1)} %bitcast.86, f32[640]{0:T(1024)S(1)} %convert_reduce_fusion.2, f32[640,1024]{1,0:T(8,128)} %get-tuple-element.75), kind=kOutput, calls=%fused_computation.40 | convolution fusion | flops 2184970240 | bytes 11569664 | tf_op jit(solution)/shard_map/dot_general | solution.py:17
  253.3 8.2 %all-to-all-start.3 = ((bf16[5,32,1792]{2,0,1:T(8,128)(2,1)}), bf16[5,32,1792]{2,0,1:T(8,128)(2,1)}, u32[]{:S(2)}, u32[]{:S(2)}) async-start(bf16[5,32,1792]{2,0,1:T(8,128)(2,1)} %copy.83), calls=%async_computation.5 | async-start | bytes 1835008 | tf_op jit(solution)/shard_map/all_to_all | solution.py:145
  261.5 10.8 %add_bitcast_fusion = f32[1,1024,1664]{2,1,0:T(8,128)} fusion(f32[1024,1664]{1,0:T(8,128)} %fusion.22, bf16[640,3456]{1,0:T(8,128)(2,1)} %bitcast.75, f32[640]{0:T(1024)S(1)} %convert_reduce_fusion.1, f32[640,1024]{1,0:T(8,128)} %get-tuple-element.74), kind=kOutput, calls=%fused_computation.1 | convolution fusion | flops 2186674176 | bytes 18385408 | tf_op jit(solution)/shard_map/dot_general | solution.py:17
  272.3 6.4 %fusion.18 = f32[1664,1024]{1,0:T(8,128)} fusion(bf16[640,1024]{1,0:T(8,128)(2,1)S(1)} %copy-done.14, bf16[640,3456]{1,0:T(8,128)(2,1)} %bitcast.87), kind=kOutput, calls=%fused_computation.36 | convolution fusion | flops 2181038080 | bytes 10256384 | tf_op jit(solution)/shard_map/dot_general | solution.py:17
  278.7 5.7 %reduce-scatter.3.cloned.1.call-done = bf16[1,160,1792]{2,1,0:T(8,128)(2,1)} async-done(((bf16[4,160,1792]{2,1,0:T(8,128)(2,1)}), bf16[1,160,1792]{2,1,0:T(8,128)(2,1)}) %reduce-scatter.3.cloned.1.call-update) | async-done | bytes 573456 | tf_op jit(solution)/shard_map/reduce_scatter | solution.py:143
  286.8 7.8 %all-to-all-start.1 = ((bf16[5,32,1792]{2,0,1:T(8,128)(2,1)}), bf16[5,32,1792]{2,0,1:T(8,128)(2,1)}, u32[]{:S(2)}, u32[]{:S(2)}) async-start(bf16[5,32,1792]{2,0,1:T(8,128)(2,1)} %copy.79), calls=%async_computation.2 | async-start | bytes 1835008 | tf_op jit(solution)/shard_map/all_to_all | solution.py:145
  294.6 9.7 %add_bitcast_fusion.1 = f32[1,1664,1024]{2,1,0:T(8,128)} fusion(f32[1664,1024]{1,0:T(8,128)} %fusion.18, bf16[640,1024]{1,0:T(8,128)(2,1)} %copy-done.12, bf16[640,3456]{1,0:T(8,128)(2,1)} %bitcast.76), kind=kOutput, calls=%fused_computation.2 | convolution fusion | flops 2182742016 | bytes 17072128 | tf_op jit(solution)/shard_map/dot_general | solution.py:17
  306.5 3.8 %all-to-all-done.1 = bf16[5,32,1792]{2,0,1:T(8,128)(2,1)} async-done(((bf16[5,32,1792]{2,0,1:T(8,128)(2,1)}), bf16[5,32,1792]{2,0,1:T(8,128)(2,1)}, u32[]{:S(2)}, u32[]{:S(2)}) %all-to-all-start.1) | async-done | bytes 573472 | tf_op jit(solution)/shard_map/all_to_all | solution.py:145
  323.6 4.9 %all-to-all-start.4 = ((f32[128,1,512]{2,1,0:T(1,128)}), f32[128,1,512]{2,1,0:T(1,128)}, u32[]{:S(2)}, u32[]{:S(2)}) async-start(f32[128,1,512]{2,1,0:T(1,128)} %bitcast.81), calls=%async_computation.6 | async-start | bytes 524288 | tf_op jit(solution)/shard_map/all_to_all | solution.py:61
  328.6 10.9 %all-to-all-done.4 = f32[128,1,512]{2,1,0:T(1,128)} async-done(((f32[128,1,512]{2,1,0:T(1,128)}), f32[128,1,512]{2,1,0:T(1,128)}, u32[]{:S(2)}, u32[]{:S(2)}) %all-to-all-start.4) | async-done | bytes 262176 | tf_op jit(solution)/shard_map/all_to_all | solution.py:61
  341.4 4.7 %all-to-all-start.5 = ((f32[128,1,512]{2,1,0:T(1,128)}), f32[128,1,512]{2,1,0:T(1,128)}, u32[]{:S(2)}, u32[]{:S(2)}) async-start(f32[128,1,512]{2,1,0:T(1,128)} %broadcast_in_dim.147), calls=%async_computation.7 | async-start | bytes 524288 | tf_op jit(solution)/shard_map/all_to_all | solution.py:66
  346.1 2.6 fusion.44
  348.7 8.5 %all-to-all-done.5 = f32[128,1,512]{2,1,0:T(1,128)} async-done(((f32[128,1,512]{2,1,0:T(1,128)}), f32[128,1,512]{2,1,0:T(1,128)}, u32[]{:S(2)}, u32[]{:S(2)}) %all-to-all-start.5) | async-done | bytes 262176 | tf_op jit(solution)/shard_map/all_to_all | solution.py:66
  358.8 2.9 reshape.157
  361.7 3.0 slice_reduce_fusion
  (101 shorter events, 57.2 us)
Async XLA Ops:
  7.2 80.9 %copy-start = (bf16[1,1664,1024]{2,1,0:T(8,128)(2,1)S(1)}, bf16[1,1664,1024]{2,1,0:T(8,128)(2,1)}, u32[]{:S(2)}) copy-start(bf16[1,1664,1024]{2,1,0:T(8,128)(2,1)} %param.16) | copy-start | bytes 10223620
  7.2 11.7 %copy-start.8 = (s32[128,2]{0,1:T(2,128)S(1)}, s32[128,2]{0,1:T(2,128)}, u32[]{:S(2)}) copy-start(s32[128,2]{0,1:T(2,128)} %param.12) | copy-start | bytes 3076
  13.6 0.8 copy-start.2
  39.2 34.5 %all-to-all-start = ((bf16[5,32,3456]{2,0,1:T(8,128)(2,1)}), bf16[5,32,3456]{2,0,1:T(8,128)(2,1)}, u32[]{:S(2)}, u32[]{:S(2)}) async-start(bf16[5,32,3456]{2,0,1:T(8,128)(2,1)} %copy.77), calls=%async_computation | async-start | bytes 3538944 | tf_op jit(solution)/shard_map/all_to_all | solution.py:113
  78.7 125.9 %all-to-all-start.2 = ((bf16[5,128,3456]{2,0,1:T(8,128)(2,1)}), bf16[5,128,3456]{2,0,1:T(8,128)(2,1)}, u32[]{:S(2)}, u32[]{:S(2)}) async-start(bf16[5,128,3456]{2,0,1:T(8,128)(2,1)} %bitcast.67), calls=%async_computation.3 | async-start | bytes 14155776 | tf_op jit(solution)/shard_map/all_to_all | solution.py:120
  84.8 140.1 %all-gather.3.cloned.1.call-start = ((), (), s32[]{:S(2)}) async-start(), calls=%async_computation.10 | async-start | bytes 5529600 | tf_op jit(solution)/shard_map/all_gather | solution.py:114
  87.4 163.5 %reduce-scatter.5.cloned.1.call-start = ((), (), s32[]{:S(2)}) async-start(), calls=%async_computation.9 | async-start | bytes 2867200 | tf_op jit(solution)/shard_map/reduce_scatter | solution.py:143
  209.4 3.3 copy-start.11
  209.9 5.3 %copy-start.4 = (bf16[4,5,32,3456]{3,2,1,0:T(8,128)(2,1)}, bf16[4,5,32,3456]{3,2,1,0:T(8,128)(2,1)S(1)}, u32[]{:S(2)}) copy-start(bf16[4,5,32,3456]{3,2,1,0:T(8,128)(2,1)S(1)} %copy.82) | copy-start | bytes 13271044
  220.2 2.8 copy-start.12
  224.6 59.9 %reduce-scatter.3.cloned.1.call-start = ((), (), s32[]{:S(2)}) async-start(), calls=%async_computation.8 | async-start | bytes 2867200 | tf_op jit(solution)/shard_map/reduce_scatter | solution.py:143
  225.9 5.4 %copy-start.9 = (bf16[20,32,3456]{2,1,0:T(8,128)(2,1)S(1)}, bf16[20,32,3456]{2,1,0:T(8,128)(2,1)}, u32[]{:S(2)}) copy-start(bf16[20,32,3456]{2,1,0:T(8,128)(2,1)} %all-gather.3.cloned.1.call-done) | copy-start | bytes 13271044
  236.2 2.8 copy-start.13
  253.3 33.5 %all-to-all-start.3 = ((bf16[5,32,1792]{2,0,1:T(8,128)(2,1)}), bf16[5,32,1792]{2,0,1:T(8,128)(2,1)}, u32[]{:S(2)}, u32[]{:S(2)}) async-start(bf16[5,32,1792]{2,0,1:T(8,128)(2,1)} %copy.83), calls=%async_computation.5 | async-start | bytes 1835008 | tf_op jit(solution)/shard_map/all_to_all | solution.py:145
  261.5 10.8 %copy-start.14 = (bf16[640,1024]{1,0:T(8,128)(2,1)S(1)}, bf16[640,1024]{1,0:T(8,128)(2,1)}, u32[]{:S(2)}) copy-start(bf16[640,1024]{1,0:T(8,128)(2,1)} %copy-done.13) | copy-start | bytes 3932164
  286.8 23.4 %all-to-all-start.1 = ((bf16[5,32,1792]{2,0,1:T(8,128)(2,1)}), bf16[5,32,1792]{2,0,1:T(8,128)(2,1)}, u32[]{:S(2)}, u32[]{:S(2)}) async-start(bf16[5,32,1792]{2,0,1:T(8,128)(2,1)} %copy.79), calls=%async_computation.2 | async-start | bytes 1835008 | tf_op jit(solution)/shard_map/all_to_all | solution.py:145
  310.2 2.8 copy-start.5
  311.6 2.5 copy-start.10
  311.6 2.6 copy-start.3
  311.6 2.9 copy-start.1
  311.6 2.9 copy-start.6
  311.6 2.9 copy-start.7
  323.6 15.8 %all-to-all-start.4 = ((f32[128,1,512]{2,1,0:T(1,128)}), f32[128,1,512]{2,1,0:T(1,128)}, u32[]{:S(2)}, u32[]{:S(2)}) async-start(f32[128,1,512]{2,1,0:T(1,128)} %bitcast.81), calls=%async_computation.6 | async-start | bytes 524288 | tf_op jit(solution)/shard_map/all_to_all | solution.py:61
  341.4 15.8 %all-to-all-start.5 = ((f32[128,1,512]{2,1,0:T(1,128)}), f32[128,1,512]{2,1,0:T(1,128)}, u32[]{:S(2)}, u32[]{:S(2)}) async-start(f32[128,1,512]{2,1,0:T(1,128)} %broadcast_in_dim.147), calls=%async_computation.7 | async-start | bytes 524288 | tf_op jit(solution)/shard_map/all_to_all | solution.py:66
Sparse Core Ops, SparseCore 0:
  87.8 108.9 all-gather.2
  224.7 26.1 reduce-scatter.4
  253.4 31.0 reduce-scatter.2

commit v6 on v5

--- a/solution.py
+++ b/solution.py
@@ -105,20 +105,12 @@
     zero = jnp.zeros((), jnp.bfloat16)
     is_hi = cols == 2 * rep_at
     is_lo = cols == 2 * rep_at + 1
-    half = capacity // 2
+    half = (3 * capacity + 4) // 5
     bounds = ((0, half), (half, capacity))
     ret_parts, in_parts, out_parts = ([], [], [])
     for chunk, (low, high) in enumerate(bounds):
-        if chunk == 0:
-            got = lax.all_to_all(send[low:high], "expert", split_axis=1, concat_axis=1, tiled=True)
-            got = lax.all_gather(got, "rep", axis=0, tiled=False)
-        else:
-            part = send[low:high]
-            wide = jnp.broadcast_to(
-                part[:, :, None], (high - low, experts, copies, part.shape[-1])
-            ).reshape(high - low, experts * copies, -1)
-            got = lax.all_to_all(wide, ("expert", "rep"), split_axis=1, concat_axis=1, tiled=True)
-            got = got.reshape(high - low, experts, copies, -1).transpose(2, 0, 1, 3)
+        got = lax.all_to_all(send[low:high], "expert", split_axis=1, concat_axis=1, tiled=True)
+        got = lax.all_gather(got, "rep", axis=0, tiled=False)
         got = got.reshape(-1, got.shape[-1])
         weight_in, weight_out, at_hi, at_lo = (w_in[0], w_out[0], is_hi, is_lo)
         if chunk:

time: 380 us -> 314 us (0.83); the launches traced: 374 us -> 312 us
  waiting for transfers between devices: 169 us -> 97.4 us
  blocking collectives: 0 us -> 53.1 us
  local copies, waits for them, and re-layouts: 58.7 us -> 34.4 us
  starting transfers between devices: 42.2 us -> 24.9 us
    all_to_all x2 -> x0, waiting for transfers between devices: 139 us -> none  [the longest x1 117 us: layer_body(): lax.all_to_all(wide, ('expert', 'rep'), split_axis=1, concat_axis=1, tile...]
    all_gather x1 -> x2, waiting for transfers between devices: 0.02 us -> 53.2 us  [layer_body(): got = lax.all_gather(got, 'rep', axis=0, tiled=False)]
    all_to_all x0 -> x2, blocking collectives: none -> 53.1 us  [layer_body(): lax.all_to_all(send[low:high], 'expert', split_axis=1, concat_axis=1, til...]
    all_to_all x2 -> x0, starting transfers between devices: 15.8 us -> none  [the longest x1 9.63 us: layer_body(): lax.all_to_all(send[low:high], 'expert', split_axis=1, concat_axis=1, til...]
    reduce_scatter x2, waiting for transfers between devices: 7.56 us -> 18.2 us  [layer_body(): back = lax.psum_scatter(packed, 'rep', scatter_dimension=0, tiled=True)]
    broadcast_in_dim x2 -> x0, local copies, waits for them, and re-layouts: 7.74 us -> none  [layer_body(): jnp.broadcast_to(part[:, :, None], (high - low, experts, copies, part.sha...]
    reshape x1 -> x0, local copies, waits for them, and re-layouts: 4.83 us -> none  [layer_body(): got = got.reshape(high - low, experts, copies, -1).transpose(2, 0, 1, 3)]
  transfers between devices with their start and end apart: 9 -> 8, of which waited for: 7 -> 6; matrix products, arithmetic and copies ran while one was open for 22% -> 23% of each run, Pallas kernels for 0% -> 0%
where the time goes in v6:
time: 314 us; the launch traced here: 312 us
  waiting for transfers between devices  97.4 us (31%)
  matrix products  65.1 us (21%)
  blocking collectives  53.1 us (17%)
  local copies, waits for them, and re-layouts  34.4 us (11%)
  starting transfers between devices  24.9 us (8%)
  other arithmetic  23.3 us (7%)
  between operations  14.1 us (4%)
    dot_general x11, matrix products, contract(): lax.dot_general(left, right, (((left_axis,), (right_axis,)), ((), ())), p...  60 us
    all_gather x2, waiting for transfers between devices, layer_body(): got = lax.all_gather(got, 'rep', axis=0, tiled=False)  53.2 us
    all_to_all x2, blocking collectives, layer_body(): lax.all_to_all(send[low:high], 'expert', split_axis=1, concat_axis=1, til...  53.1 us
    reduce_scatter x2, waiting for transfers between devices, layer_body(): back = lax.psum_scatter(packed, 'rep', scatter_dimension=0, tiled=True)  18.2 us
    all_to_all x2, starting transfers between devices, layer_body(): lax.all_to_all(back, 'expert', split_axis=1, concat_axis=1, tiled=True)  15.7 us
    all_to_all x1, waiting for transfers between devices, all_sum(): lax.all_to_all(flat.reshape(devices, width), ('expert', 'rep'), split_axi...  11.3 us
    all_to_all x1, waiting for transfers between devices, all_sum(): lax.all_to_all(spread_out, ('expert', 'rep'), split_axis=0, concat_axis=0...  8.31 us
    all_to_all x2, waiting for transfers between devices, layer_body(): lax.all_to_all(back, 'expert', split_axis=1, concat_axis=1, tiled=True)  6.38 us
  transfers between devices with their start and end apart: 8, of which 6 were waited for; matrix products, arithmetic and copies ran while one was open for 23% of the time, Pallas kernels for 0%

profile of v6, /device:TPU:1, one launch (start us, length us, event | category | flops | bytes accessed | tf_op | source)
XLA Modules:
  0.0 312.3 jit_solution(9414895854474432698)
XLA Ops:
  24.1 3.3 %gather_fusion = bf16[128,1664]{1,0:T(8,128)(2,1)} fusion(bf16[2,256,1664]{2,1,0:T(8,128)(2,1)} %param.10, s32[128]{0:T(128)S(1)} %reshape.150), kind=kCustom, calls=%fused_computation | custom fusion | bytes 852992 | tf_op jit(solution)/shard_map/jit(take_along_axis)/gather | solution.py:79
  28.6 3.1 %convolution_convert_fusion = bf16[320,3328]{1,0:T(8,128)(2,1)} fusion(bf16[128,1664]{1,0:T(8,128)(2,1)S(1)} %broadcast_select_fusion, bf16[128,1664]{1,0:T(8,128)(2,1)} %copy-done.3, f32[128,320]{0,1:T(8,128)} %convert_reduce_fusion.2), kind=kOutput, calls=%fused_computation.3 | convolution fusion | flops 275439616 | bytes 3145728 | tf_op jit(solution)/shard_map/dot_general | solution.py:17
  31.7 4.5 %concatenate.19 = bf16[320,3456]{1,0:T(8,128)(2,1)} concatenate(bf16[320,3328]{1,0:T(8,128)(2,1)} %convolution_convert_fusion, bf16[320,1]{1,0:T(8,128)(2,1)} %broadcast_in_dim.154, bf16[320,127]{1,0:T(8,128)(2,1)S(1)} %broadcast_in_dim.136), dimensions={1} | concatenate | bytes 4423680 | tf_op jit(solution)/shard_map/concatenate | solution.py:101
  38.0 24.6 %all_to_all.35 = bf16[4,32,3456]{2,0,1:T(4,128)(2,1)S(1)} all-to-all(bf16[4,32,3456]{2,0,1:T(4,128)(2,1)S(1)} %copy.77), channel_id=1, replica_groups=mesh['expert'=32,'rep'=4] {'expert'}, dimensions={1} | all-to-all | bytes 1769472 | tf_op jit(solution)/shard_map/all_to_all | solution.py:112
  65.4 28.5 %all_to_all.36 = bf16[6,32,3456]{2,0,1:T(8,128)(2,1)S(1)} all-to-all(bf16[6,32,3456]{2,0,1:T(8,128)(2,1)S(1)} %copy.74), channel_id=1, replica_groups=mesh['expert'=32,'rep'=4] {'expert'}, dimensions={1} | all-to-all | bytes 2654208 | tf_op jit(solution)/shard_map/all_to_all | solution.py:112
  95.2 8.6 %all-gather.7.cloned.1.call-done = bf16[16,32,3456]{2,1,0:T(8,128)(2,1)} async-done(((bf16[4,32,3456]{2,1,0:T(8,128)(2,1)}), bf16[16,32,3456]{2,1,0:T(8,128)(2,1)}) %all-gather.7.cloned.1.call-update) | async-done | bytes 3538960 | tf_op jit(solution)/shard_map/all_gather | solution.py:113
  104.8 4.6 %fusion.25 = f32[512,1024]{1,0:T(8,128)S(1)} fusion(bf16[1024,1664]{1,0:T(8,128)(2,1)} %bitcast.84, bf16[512,3456]{1,0:T(8,128)(2,1)} %bitcast.70), kind=kOutput, calls=%fused_computation.42 | convolution fusion | flops 1744830464 | bytes 7208960 | tf_op jit(solution)/shard_map/dot_general | solution.py:17
  109.4 5.7 %fusion.19 = (bf16[512,1024]{1,0:T(8,128)(2,1)S(1)}, f32[512]{0:T(512)S(1)}, f32[512,1024]{1,0:T(8,128)}) fusion(f32[512,1024]{1,0:T(8,128)S(1)} %fusion.25, f32[512]{0:T(512)S(1)} %convert_reduce_fusion.3, bf16[1664,1024]{1,0:T(8,128)(2,1)S(1)} %bitcast.61, bf16[512,3456]{1,0:T(8,128)(2,1)} %bitcast.71), kind=kOutput, calls=%fused_computation.32 | convolution fusion | flops 1752169984 | bytes 10358784 | tf_op jit(solution)/shard_map/dot_general | solution.py:17
  115.3 2.1 convolution_convert_fusion.2
  119.2 44.6 %all-gather.5.cloned.1.call-done = bf16[24,32,3456]{2,1,0:T(8,128)(2,1)} async-done(((bf16[6,32,3456]{2,1,0:T(8,128)(2,1)}), bf16[24,32,3456]{2,1,0:T(8,128)(2,1)}) %all-gather.5.cloned.1.call-update) | async-done | bytes 5308432 | tf_op jit(solution)/shard_map/all_gather | solution.py:113
  164.8 5.8 %fusion.12 = f32[768,1024]{1,0:T(8,128)S(1)} fusion(bf16[768,3456]{1,0:T(8,128)(2,1)} %bitcast.77, bf16[1,1024,1664]{2,1,0:T(8,128)(2,1)} %param.17), kind=kOutput, calls=%fused_computation.25 | convolution fusion | flops 2617245696 | bytes 9109504 | tf_op jit(solution)/shard_map/dot_general | solution.py:17
  170.6 6.9 %fusion.5 = (bf16[768,1024]{1,0:T(8,128)(2,1)S(1)}, f32[768]{0:T(1024)S(1)}, f32[768,1024]{1,0:T(8,128)}) fusion(f32[768,1024]{1,0:T(8,128)S(1)} %fusion.12, f32[768]{0:T(1024)S(1)} %convert_reduce_fusion.1, bf16[1,1664,1024]{2,1,0:T(8,128)(2,1)S(1)} %copy-done, bf16[768,3456]{1,0:T(8,128)(2,1)} %bitcast.78), kind=kOutput, calls=%fused_computation.11 | convolution fusion | flops 2628254976 | bytes 13834240 | tf_op jit(solution)/shard_map/dot_general | solution.py:17
  177.8 3.3 %convolution_convert_fusion.1 = bf16[768,1664]{1,0:T(8,128)(2,1)S(1)} fusion(bf16[768,1024]{1,0:T(8,128)(2,1)S(1)} %get-tuple-element.66, bf16[1,1664,1024]{2,1,0:T(8,128)(2,1)S(1)} %copy-done), kind=kOutput, calls=%fused_computation.5 | convolution fusion | flops 2618523648 | bytes 7536640 | tf_op jit(solution)/shard_map/dot_general | solution.py:17
  183.0 6.3 %fusion.10 = f32[1024,1664]{1,0:T(8,128)S(1)} fusion(bf16[768,3456]{1,0:T(8,128)(2,1)} %bitcast.79, f32[768]{0:T(1024)S(1)} %convert_reduce_fusion.1, f32[768,1024]{1,0:T(8,128)} %get-tuple-element.73), kind=kOutput, calls=%fused_computation.23 | convolution fusion | flops 2621964288 | bytes 12520448 | tf_op jit(solution)/shard_map/dot_general | solution.py:17
  189.3 5.8 %add_bitcast_fusion = f32[1,1024,1664]{2,1,0:T(8,128)} fusion(f32[1024,1664]{1,0:T(8,128)S(1)} %fusion.10, bf16[512,3456]{1,0:T(8,128)(2,1)} %bitcast.72, f32[512]{0:T(512)S(1)} %convert_reduce_fusion.3, f32[512,1024]{1,0:T(8,128)S(1)} %copy-done.11), kind=kOutput, calls=%fused_computation.1 | convolution fusion | flops 1749680128 | bytes 17434624 | tf_op jit(solution)/shard_map/dot_general | solution.py:17
  195.1 2.1 copy.79
  197.2 7.9 %all-to-all-start.3 = ((bf16[4,32,1792]{2,0,1:T(4,128)(2,1)}), bf16[4,32,1792]{2,0,1:T(4,128)(2,1)S(1)}, u32[]{:S(2)}, u32[]{:S(2)}) async-start(bf16[4,32,1792]{2,0,1:T(4,128)(2,1)} %copy.79), calls=%async_computation.5 | async-start | bytes 917504 | tf_op jit(solution)/shard_map/all_to_all | solution.py:137
  205.1 8.1 %fusion.6 = f32[1664,1024]{1,0:T(8,128)} fusion(bf16[768,1024]{1,0:T(8,128)(2,1)} %copy-done.12, bf16[768,3456]{1,0:T(8,128)(2,1)} %bitcast.80), kind=kOutput, calls=%fused_computation.19 | convolution fusion | flops 2617245696 | bytes 10944512 | tf_op jit(solution)/shard_map/dot_general | solution.py:17
  213.3 18.1 %reduce-scatter.3.cloned.1.call-done = bf16[1,192,1792]{2,1,0:T(8,128)(2,1)} async-done(((bf16[4,192,1792]{2,1,0:T(8,128)(2,1)}), bf16[1,192,1792]{2,1,0:T(8,128)(2,1)}) %reduce-scatter.3.cloned.1.call-update) | async-done | bytes 688144 | tf_op jit(solution)/shard_map/reduce_scatter | solution.py:135
  231.4 2.4 copy.76
  233.8 7.8 %all-to-all-start.1 = ((bf16[6,32,1792]{2,0,1:T(8,128)(2,1)}), bf16[6,32,1792]{2,0,1:T(8,128)(2,1)S(1)}, u32[]{:S(2)}, u32[]{:S(2)}) async-start(bf16[6,32,1792]{2,0,1:T(8,128)(2,1)} %copy.76), calls=%async_computation.2 | async-start | bytes 1835008 | tf_op jit(solution)/shard_map/all_to_all | solution.py:137
  241.6 8.3 %add_bitcast_fusion.1 = f32[1,1664,1024]{2,1,0:T(8,128)} fusion(f32[1664,1024]{1,0:T(8,128)} %fusion.6, bf16[512,1024]{1,0:T(8,128)(2,1)S(1)} %copy-done.7, bf16[512,3456]{1,0:T(8,128)(2,1)} %bitcast.73), kind=kOutput, calls=%fused_computation.2 | convolution fusion | flops 1746534400 | bytes 16384000 | tf_op jit(solution)/shard_map/dot_general | solution.py:17
  250.8 6.4 %all-to-all-done.1 = bf16[6,32,1792]{2,0,1:T(8,128)(2,1)S(1)} async-done(((bf16[6,32,1792]{2,0,1:T(8,128)(2,1)}), bf16[6,32,1792]{2,0,1:T(8,128)(2,1)S(1)}, u32[]{:S(2)}, u32[]{:S(2)}) %all-to-all-start.1) | async-done | bytes 688160 | tf_op jit(solution)/shard_map/all_to_all | solution.py:137
  260.0 2.0 fusion.45
  263.8 4.2 %all-to-all-start.4 = ((f32[128,1,512]{2,1,0:T(1,128)}), f32[128,1,512]{2,1,0:T(1,128)S(1)}, u32[]{:S(2)}, u32[]{:S(2)}) async-start(f32[128,1,512]{2,1,0:T(1,128)} %bitcast.20), calls=%async_computation.6 | async-start | bytes 524288 | tf_op jit(solution)/shard_map/all_to_all | solution.py:61
  268.0 11.3 %all-to-all-done.4 = f32[128,1,512]{2,1,0:T(1,128)S(1)} async-done(((f32[128,1,512]{2,1,0:T(1,128)}), f32[128,1,512]{2,1,0:T(1,128)S(1)}, u32[]{:S(2)}, u32[]{:S(2)}) %all-to-all-start.4) | async-done | bytes 262176 | tf_op jit(solution)/shard_map/all_to_all | solution.py:61
  280.4 4.7 %all-to-all-start.5 = ((f32[128,1,512]{2,1,0:T(1,128)}), f32[128,1,512]{2,1,0:T(1,128)}, u32[]{:S(2)}, u32[]{:S(2)}) async-start(f32[128,1,512]{2,1,0:T(1,128)} %broadcast_in_dim.153), calls=%async_computation.7 | async-start | bytes 524288 | tf_op jit(solution)/shard_map/all_to_all | solution.py:66
  285.1 2.8 fusion.44
  287.8 8.3 %all-to-all-done.5 = f32[128,1,512]{2,1,0:T(1,128)} async-done(((f32[128,1,512]{2,1,0:T(1,128)}), f32[128,1,512]{2,1,0:T(1,128)}, u32[]{:S(2)}, u32[]{:S(2)}) %all-to-all-start.5) | async-done | bytes 262176 | tf_op jit(solution)/shard_map/all_to_all | solution.py:66
  297.8 2.9 reshape.147
  300.7 3.0 slice_reduce_fusion
  303.7 2.1 copy.84
  (98 shorter events, 38.0 us)
Async XLA Ops:
  7.2 88.0 %copy-start = (bf16[1,1664,1024]{2,1,0:T(8,128)(2,1)S(1)}, bf16[1,1664,1024]{2,1,0:T(8,128)(2,1)}, u32[]{:S(2)}) copy-start(bf16[1,1664,1024]{2,1,0:T(8,128)(2,1)} %param.16) | copy-start | bytes 10223620
  7.2 96.6 %all-gather.7.cloned.1.call-start = ((), (), s32[]{:S(2)}) async-start(), calls=%async_computation.11 | async-start | bytes 4423680 | tf_op jit(solution)/shard_map/all_gather | solution.py:113
  13.6 0.8 copy-start.3
  63.6 100.1 %all-gather.5.cloned.1.call-start = ((), (), s32[]{:S(2)}) async-start(), calls=%async_computation.10 | async-start | bytes 6635520 | tf_op jit(solution)/shard_map/all_gather | solution.py:113
  63.6 1.3 slice-start
  95.1 100.0 %reduce-scatter.5.cloned.1.call-start = ((), (), s32[]{:S(2)}) async-start(), calls=%async_computation.9 | async-start | bytes 2293760 | tf_op jit(solution)/shard_map/reduce_scatter | solution.py:135
  115.1 2.3 copy-start.6
  118.9 112.5 %reduce-scatter.3.cloned.1.call-start = ((), (), s32[]{:S(2)}) async-start(), calls=%async_computation.8 | async-start | bytes 3440640 | tf_op jit(solution)/shard_map/reduce_scatter | solution.py:135
  177.5 3.6 %copy-start.12 = (bf16[768,1024]{1,0:T(8,128)(2,1)}, bf16[768,1024]{1,0:T(8,128)(2,1)S(1)}, u32[]{:S(2)}) copy-start(bf16[768,1024]{1,0:T(8,128)(2,1)S(1)} %get-tuple-element.66) | copy-start | bytes 4718596
  181.1 1.8 copy-start.10
  183.0 6.3 %copy-start.11 = (f32[512,1024]{1,0:T(8,128)S(1)}, f32[512,1024]{1,0:T(8,128)}, u32[]{:S(2)}) copy-start(f32[512,1024]{1,0:T(8,128)} %get-tuple-element.72) | copy-start | bytes 6291460
  197.2 36.6 %all-to-all-start.3 = ((bf16[4,32,1792]{2,0,1:T(4,128)(2,1)}), bf16[4,32,1792]{2,0,1:T(4,128)(2,1)S(1)}, u32[]{:S(2)}, u32[]{:S(2)}) async-start(bf16[4,32,1792]{2,0,1:T(4,128)(2,1)} %copy.79), calls=%async_computation.5 | async-start | bytes 917504 | tf_op jit(solution)/shard_map/all_to_all | solution.py:137
  213.3 28.3 %copy-start.7 = (bf16[512,1024]{1,0:T(8,128)(2,1)S(1)}, bf16[512,1024]{1,0:T(8,128)(2,1)}, u32[]{:S(2)}) copy-start(bf16[512,1024]{1,0:T(8,128)(2,1)} %copy-done.6) | copy-start | bytes 3145732
  233.8 23.3 %all-to-all-start.1 = ((bf16[6,32,1792]{2,0,1:T(8,128)(2,1)}), bf16[6,32,1792]{2,0,1:T(8,128)(2,1)S(1)}, u32[]{:S(2)}, u32[]{:S(2)}) async-start(bf16[6,32,1792]{2,0,1:T(8,128)(2,1)} %copy.76), calls=%async_computation.2 | async-start | bytes 1835008 | tf_op jit(solution)/shard_map/all_to_all | solution.py:137
  249.9 8.6 %copy-start.5 = (f32[128,320]{0,1:T(8,128)S(1)}, f32[128,320]{0,1:T(8,128)}, u32[]{:S(2)}) copy-start(f32[128,320]{0,1:T(8,128)} %convert_reduce_fusion.2) | copy-start | bytes 491524
  250.7 8.9 %copy-start.4 = (bf16[128,1664]{1,0:T(8,128)(2,1)S(1)}, bf16[128,1664]{1,0:T(8,128)(2,1)}, u32[]{:S(2)}) copy-start(bf16[128,1664]{1,0:T(8,128)(2,1)} %copy-done.3) | copy-start | bytes 1277956
  250.7 9.2 %copy-start.2 = (bf16[128,1664]{1,0:T(8,128)(2,1)S(1)}, bf16[128,1664]{1,0:T(8,128)(2,1)}, u32[]{:S(2)}) copy-start(bf16[128,1664]{1,0:T(8,128)(2,1)} %param.9) | copy-start | bytes 1277956
  250.8 9.2 %copy-start.8 = (f32[1664,32]{0,1:T(8,128)S(1)}, f32[1664,32]{0,1:T(8,128)}, u32[]{:S(2)}) copy-start(f32[1664,32]{0,1:T(8,128)} %param.15) | copy-start | bytes 638980
  250.8 9.2 %copy-start.9 = (f32[1664]{0:T(1024)S(1)}, f32[1664]{0:T(1024)}, u32[]{:S(2)}) copy-start(f32[1664]{0:T(1024)} %param.13) | copy-start | bytes 19972
  263.8 15.5 %all-to-all-start.4 = ((f32[128,1,512]{2,1,0:T(1,128)}), f32[128,1,512]{2,1,0:T(1,128)S(1)}, u32[]{:S(2)}, u32[]{:S(2)}) async-start(f32[128,1,512]{2,1,0:T(1,128)} %bitcast.20), calls=%async_computation.6 | async-start | bytes 524288 | tf_op jit(solution)/shard_map/all_to_all | solution.py:61
  280.4 15.8 %all-to-all-start.5 = ((f32[128,1,512]{2,1,0:T(1,128)}), f32[128,1,512]{2,1,0:T(1,128)}, u32[]{:S(2)}, u32[]{:S(2)}) async-start(f32[128,1,512]{2,1,0:T(1,128)} %broadcast_in_dim.153), calls=%async_computation.7 | async-start | bytes 524288 | tf_op jit(solution)/shard_map/all_to_all | solution.py:66
  285.1 20.7 %copy-start.1 = (bf16[1,1664,1024]{2,1,0:T(8,128)(2,1)S(1)}, bf16[1,1664,1024]{2,1,0:T(8,128)(2,1)}, u32[]{:S(2)}) copy-start(bf16[1,1664,1024]{2,1,0:T(8,128)(2,1)} %param.16) | copy-start | bytes 10223620
Sparse Core Ops, SparseCore 0:
  63.7 40.0 all-gather.6
  106.0 57.6 all-gather.4
  166.2 28.1 reduce-scatter.4
  196.6 34.7 reduce-scatter.2

commit v7 on v6

--- a/solution.py
+++ b/solution.py
@@ -91,25 +91,33 @@
     assign = jnp.sum(spread, axis=1)
     assign_half = assign.astype(jnp.bfloat16)
     both = jnp.concatenate([normed_in, grad_kept], axis=1)
-    send_rows = contract(assign_half, both, 0, 0).astype(jnp.bfloat16)
     send_gate = jnp.einsum(
         "tks,tk->s", spread, gate_half.astype(jnp.float32), precision=PRECISE
     ).astype(jnp.bfloat16)
-    gate_block = jnp.concatenate(
-        [send_gate[:, None], jnp.zeros((experts * capacity, lane - 1), jnp.bfloat16)], axis=1
-    )
-    send = jnp.concatenate([send_rows, gate_block], axis=1).reshape(capacity, experts, -1)
+
+    def send_part(low, high):
+        rows = contract(assign_half[:, low * experts : high * experts], both, 0, 0)
+        part_gate = send_gate[low * experts : high * experts]
+        gate_block = jnp.concatenate(
+            [part_gate[:, None], jnp.zeros((part_gate.shape[0], lane - 1), jnp.bfloat16)],
+            axis=1,
+        )
+        whole = jnp.concatenate([rows.astype(jnp.bfloat16), gate_block], axis=1)
+        return whole.reshape(high - low, experts, -1)
+
     rep_at = lax.axis_index("rep")
     copies = lax.axis_size("rep")
     cols = jnp.arange(lane, dtype=jnp.int32)[None, :]
     zero = jnp.zeros((), jnp.bfloat16)
     is_hi = cols == 2 * rep_at
     is_lo = cols == 2 * rep_at + 1
-    half = (3 * capacity + 4) // 5
+    half = capacity // 2
     bounds = ((0, half), (half, capacity))
     ret_parts, in_parts, out_parts = ([], [], [])
     for chunk, (low, high) in enumerate(bounds):
-        got = lax.all_to_all(send[low:high], "expert", split_axis=1, concat_axis=1, tiled=True)
+        got = lax.all_to_all(
+            send_part(low, high), "expert", split_axis=1, concat_axis=1, tiled=True
+        )
         got = lax.all_gather(got, "rep", axis=0, tiled=False)
         got = got.reshape(-1, got.shape[-1])
         weight_in, weight_out, at_hi, at_lo = (w_in[0], w_out[0], is_hi, is_lo)

time: 314 us -> 327 us (1.041); the launches traced: 312 us -> 320 us
  blocking collectives: 53.1 us -> 62.9 us
  waiting for transfers between devices: 97.4 us -> 88.1 us
  local copies, waits for them, and re-layouts: 34.4 us -> 42.8 us
    all_to_all x2, blocking collectives: 53.1 us -> 62.9 us  [layer_body(): lax.all_to_all(send_part(low, high), 'expert', split_axis=1, concat_axis=...]
    all_gather x2, waiting for transfers between devices: 53.2 us -> 44 us  [layer_body(): got = lax.all_gather(got, 'rep', axis=0, tiled=False)]
    concatenate x1 -> x5, local copies, waits for them, and re-layouts: 4.55 us -> 11.1 us  [send_part(): whole = jnp.concatenate([rows.astype(jnp.bfloat16), gate_block], axis=1)]
    dot_general x11 -> x12, matrix products: 60 us -> 60 us  [contract(): lax.dot_general(left, right, (((left_axis,), (right_axis,)), ((), ())), p...]
  transfers between devices with their start and end apart: 8 -> 8, of which waited for: 6 -> 7; matrix products, arithmetic and copies ran while one was open for 23% -> 25% of each run, Pallas kernels for 0% -> 0%
where the time goes in v7:
time: 327 us; the launch traced here: 320 us
  waiting for transfers between devices  88.1 us (27%)
  matrix products  65.1 us (20%)
  blocking collectives  62.9 us (19%)
  local copies, waits for them, and re-layouts  42.8 us (13%)
  starting transfers between devices  25.6 us (8%)
  other arithmetic  21.2 us (6%)
  between operations  14.6 us (4%)
    all_to_all x2, blocking collectives, layer_body(): lax.all_to_all(send_part(low, high), 'expert', split_axis=1, concat_axis=...  62.9 us
    dot_general x12, matrix products, contract(): lax.dot_general(left, right, (((left_axis,), (right_axis,)), ((), ())), p...  60 us
    all_gather x2, waiting for transfers between devices, layer_body(): got = lax.all_gather(got, 'rep', axis=0, tiled=False)  44 us
    reduce_scatter x2, waiting for transfers between devices, layer_body(): back = lax.psum_scatter(packed, 'rep', scatter_dimension=0, tiled=True)  16.5 us
    all_to_all x2, starting transfers between devices, layer_body(): lax.all_to_all(back, 'expert', split_axis=1, concat_axis=1, tiled=True)  15.9 us
    all_to_all x1, waiting for transfers between devices, all_sum(): lax.all_to_all(flat.reshape(devices, width), ('expert', 'rep'), split_axi...  11.3 us
    concatenate x5, local copies, waits for them, and re-layouts, send_part(): whole = jnp.concatenate([rows.astype(jnp.bfloat16), gate_block], axis=1)  11.1 us
    all_to_all x1, waiting for transfers between devices, all_sum(): lax.all_to_all(spread_out, ('expert', 'rep'), split_axis=0, concat_axis=0...  8.3 us
  transfers between devices with their start and end apart: 8, of which 7 were waited for; matrix products, arithmetic and copies ran while one was open for 25% of the time, Pallas kernels for 0%

profile of v7, /device:TPU:1, one launch (start us, length us, event | category | flops | bytes accessed | tf_op | source)
XLA Modules:
  0.0 320.1 jit_solution(4291685810733695131)
XLA Ops:
  24.4 3.3 %gather_fusion = bf16[128,1664]{1,0:T(8,128)(2,1)} fusion(bf16[2,256,1664]{2,1,0:T(8,128)(2,1)} %param.10, s32[128]{0:T(128)S(1)} %reshape.169), kind=kCustom, calls=%fused_computation | custom fusion | bytes 852992 | tf_op jit(solution)/shard_map/jit(take_along_axis)/gather | solution.py:79
  32.9 3.7 %concatenate.32 = bf16[5,32,3456]{2,0,1:T(8,128)(2,1)} concatenate(bf16[5,32,3328]{2,0,1:T(8,128)(2,1)} %copy.78, bf16[5,32,1]{2,0,1:T(8,128)(2,1)} %copy.79, bf16[5,32,127]{2,0,1:T(8,128)(2,1)S(1)} %concatenate.31), dimensions={2} | concatenate | bytes 2211840 | tf_op jit(solution)/shard_map/concatenate | solution.py:105
  36.6 34.4 %all_to_all.35 = bf16[5,32,3456]{2,0,1:T(8,128)(2,1)S(1)} all-to-all(bf16[5,32,3456]{2,0,1:T(8,128)(2,1)} %concatenate.32), channel_id=1, replica_groups=mesh['expert'=32,'rep'=4] {'expert'}, dimensions={1} | all-to-all | bytes 2211840 | tf_op jit(solution)/shard_map/all_to_all | solution.py:118
  78.4 3.8 %concatenate.35 = bf16[5,32,3456]{2,0,1:T(8,128)(2,1)} concatenate(bf16[5,32,3328]{2,0,1:T(8,128)(2,1)} %copy.82, bf16[5,32,1]{2,0,1:T(8,128)(2,1)S(1)} %copy-done.8, bf16[5,32,127]{2,0,1:T(8,128)(2,1)S(1)} %concatenate.31), dimensions={2} | concatenate | bytes 2211840 | tf_op jit(solution)/shard_map/concatenate | solution.py:105
  82.2 28.5 %all_to_all.36 = bf16[5,32,3456]{2,0,1:T(8,128)(2,1)S(1)} all-to-all(bf16[5,32,3456]{2,0,1:T(8,128)(2,1)} %concatenate.35), channel_id=1, replica_groups=mesh['expert'=32,'rep'=4] {'expert'}, dimensions={1} | all-to-all | bytes 2211840 | tf_op jit(solution)/shard_map/all_to_all | solution.py:118
  112.3 7.3 %all-gather.5.cloned.1.call-done = bf16[20,32,3456]{2,1,0:T(8,128)(2,1)} async-done(((bf16[5,32,3456]{2,1,0:T(8,128)(2,1)}), bf16[20,32,3456]{2,1,0:T(8,128)(2,1)}) %all-gather.5.cloned.1.call-update) | async-done | bytes 4423696 | tf_op jit(solution)/shard_map/all_gather | solution.py:121
  120.7 5.3 %fusion.24 = f32[640,1024]{1,0:T(8,128)S(1)} fusion(bf16[640,3456]{1,0:T(8,128)(2,1)} %bitcast.72, bf16[1,1024,1664]{2,1,0:T(8,128)(2,1)} %param.17), kind=kOutput, calls=%fused_computation.42 | convolution fusion | flops 2181038080 | bytes 8159232 | tf_op jit(solution)/shard_map/dot_general | solution.py:17
  126.1 4.9 %fusion.5 = (bf16[640,1024]{1,0:T(8,128)(2,1)S(1)}, f32[640]{0:T(1024)S(1)}, f32[640,1024]{1,0:T(8,128)}) fusion(f32[640,1024]{1,0:T(8,128)S(1)} %fusion.24, f32[640]{0:T(1024)S(1)} %convert_reduce_fusion.2, bf16[1,1664,1024]{2,1,0:T(8,128)(2,1)S(1)} %copy-done, bf16[640,3456]{1,0:T(8,128)(2,1)S(1)} %bitcast.75), kind=kOutput, calls=%fused_computation.14 | convolution fusion | flops 2190212608 | bytes 12098048 | tf_op jit(solution)/shard_map/dot_general | solution.py:17
  131.2 2.6 convolution_convert_fusion.3
  135.7 36.7 %all-gather.7.cloned.1.call-done = bf16[20,32,3456]{2,1,0:T(8,128)(2,1)} async-done(((bf16[5,32,3456]{2,1,0:T(8,128)(2,1)}), bf16[20,32,3456]{2,1,0:T(8,128)(2,1)}) %all-gather.7.cloned.1.call-update) | async-done | bytes 4423696 | tf_op jit(solution)/shard_map/all_gather | solution.py:121
  173.5 5.3 %fusion.16 = f32[640,1024]{1,0:T(8,128)S(1)} fusion(bf16[1024,1664]{1,0:T(8,128)(2,1)} %bitcast.84, bf16[640,3456]{1,0:T(8,128)(2,1)} %bitcast.77), kind=kOutput, calls=%fused_computation.34 | convolution fusion | flops 2181038080 | bytes 8159232 | tf_op jit(solution)/shard_map/dot_general | solution.py:17
  178.8 4.9 %fusion.11 = (bf16[640,1024]{1,0:T(8,128)(2,1)S(1)}, f32[640]{0:T(1024)S(1)}, f32[640,1024]{1,0:T(8,128)}) fusion(f32[640,1024]{1,0:T(8,128)S(1)} %fusion.16, f32[640]{0:T(1024)S(1)} %convert_reduce_fusion.1, bf16[1664,1024]{1,0:T(8,128)(2,1)S(1)} %bitcast.61, bf16[640,3456]{1,0:T(8,128)(2,1)S(1)} %bitcast.80), kind=kOutput, calls=%fused_computation.20 | convolution fusion | flops 2190212608 | bytes 12098048 | tf_op jit(solution)/shard_map/dot_general | solution.py:17
  183.9 2.6 convolution_convert_fusion.2
  189.1 6.8 %fusion.22 = f32[1024,1664]{1,0:T(8,128)} fusion(bf16[640,3456]{1,0:T(8,128)(2,1)} %bitcast.73, f32[640]{0:T(1024)S(1)} %convert_reduce_fusion.2, f32[640,1024]{1,0:T(8,128)S(1)} %copy-done.24), kind=kOutput, calls=%fused_computation.40 | convolution fusion | flops 2184970240 | bytes 11569664 | tf_op jit(solution)/shard_map/dot_general | solution.py:17
  195.9 10.7 %reduce-scatter.3.cloned.1.call-done = bf16[1,160,1792]{2,1,0:T(8,128)(2,1)} async-done(((bf16[4,160,1792]{2,1,0:T(8,128)(2,1)}), bf16[1,160,1792]{2,1,0:T(8,128)(2,1)}) %reduce-scatter.3.cloned.1.call-update) | async-done | bytes 573456 | tf_op jit(solution)/shard_map/reduce_scatter | solution.py:143
  206.6 2.3 copy.81
  208.9 8.1 %all-to-all-start.1 = ((bf16[5,32,1792]{2,0,1:T(8,128)(2,1)}), bf16[5,32,1792]{2,0,1:T(8,128)(2,1)S(1)}, u32[]{:S(2)}, u32[]{:S(2)}) async-start(bf16[5,32,1792]{2,0,1:T(8,128)(2,1)} %copy.81), calls=%async_computation.2 | async-start | bytes 1835008 | tf_op jit(solution)/shard_map/all_to_all | solution.py:145
  217.0 10.8 %add_bitcast_fusion = f32[1,1024,1664]{2,1,0:T(8,128)} fusion(f32[1024,1664]{1,0:T(8,128)} %fusion.22, bf16[640,3456]{1,0:T(8,128)(2,1)} %bitcast.78, f32[640]{0:T(1024)S(1)} %convert_reduce_fusion.1, f32[640,1024]{1,0:T(8,128)} %get-tuple-element.74), kind=kOutput, calls=%fused_computation.1 | convolution fusion | flops 2186674176 | bytes 18385408 | tf_op jit(solution)/shard_map/dot_general | solution.py:17
  227.8 6.4 %fusion.18 = f32[1664,1024]{1,0:T(8,128)} fusion(bf16[640,1024]{1,0:T(8,128)(2,1)S(1)} %copy-done.28, bf16[640,3456]{1,0:T(8,128)(2,1)} %bitcast.74), kind=kOutput, calls=%fused_computation.36 | convolution fusion | flops 2181038080 | bytes 10256384 | tf_op jit(solution)/shard_map/dot_general | solution.py:17
  234.2 5.7 %reduce-scatter.5.cloned.1.call-done = bf16[1,160,1792]{2,1,0:T(8,128)(2,1)} async-done(((bf16[4,160,1792]{2,1,0:T(8,128)(2,1)}), bf16[1,160,1792]{2,1,0:T(8,128)(2,1)}) %reduce-scatter.5.cloned.1.call-update) | async-done | bytes 573456 | tf_op jit(solution)/shard_map/reduce_scatter | solution.py:143
  240.0 2.3 copy.85
  242.3 7.8 %all-to-all-start.3 = ((bf16[5,32,1792]{2,0,1:T(8,128)(2,1)}), bf16[5,32,1792]{2,0,1:T(8,128)(2,1)S(1)}, u32[]{:S(2)}, u32[]{:S(2)}) async-start(bf16[5,32,1792]{2,0,1:T(8,128)(2,1)} %copy.85), calls=%async_computation.5 | async-start | bytes 1835008 | tf_op jit(solution)/shard_map/all_to_all | solution.py:145
  250.1 7.5 %add_bitcast_fusion.1 = f32[1,1664,1024]{2,1,0:T(8,128)} fusion(f32[1664,1024]{1,0:T(8,128)} %fusion.18, bf16[640,1024]{1,0:T(8,128)(2,1)S(1)} %copy-done.26, bf16[640,3456]{1,0:T(8,128)(2,1)} %bitcast.79), kind=kOutput, calls=%fused_computation.2 | convolution fusion | flops 2182742016 | bytes 17072128 | tf_op jit(solution)/shard_map/dot_general | solution.py:17
  257.7 7.9 %all-to-all-done.3 = bf16[5,32,1792]{2,0,1:T(8,128)(2,1)S(1)} async-done(((bf16[5,32,1792]{2,0,1:T(8,128)(2,1)}), bf16[5,32,1792]{2,0,1:T(8,128)(2,1)S(1)}, u32[]{:S(2)}, u32[]{:S(2)}) %all-to-all-start.3) | async-done | bytes 573472 | tf_op jit(solution)/shard_map/all_to_all | solution.py:145
  271.4 4.2 %all-to-all-start.4 = ((f32[128,1,512]{2,1,0:T(1,128)}), f32[128,1,512]{2,1,0:T(1,128)S(1)}, u32[]{:S(2)}, u32[]{:S(2)}) async-start(f32[128,1,512]{2,1,0:T(1,128)} %bitcast.20), calls=%async_computation.6 | async-start | bytes 524288 | tf_op jit(solution)/shard_map/all_to_all | solution.py:61
  275.6 11.3 %all-to-all-done.4 = f32[128,1,512]{2,1,0:T(1,128)S(1)} async-done(((f32[128,1,512]{2,1,0:T(1,128)}), f32[128,1,512]{2,1,0:T(1,128)S(1)}, u32[]{:S(2)}, u32[]{:S(2)}) %all-to-all-start.4) | async-done | bytes 262176 | tf_op jit(solution)/shard_map/all_to_all | solution.py:61
  288.0 4.7 %all-to-all-start.5 = ((f32[128,1,512]{2,1,0:T(1,128)}), f32[128,1,512]{2,1,0:T(1,128)}, u32[]{:S(2)}, u32[]{:S(2)}) async-start(f32[128,1,512]{2,1,0:T(1,128)} %broadcast_in_dim.131), calls=%async_computation.7 | async-start | bytes 524288 | tf_op jit(solution)/shard_map/all_to_all | solution.py:66
  292.7 2.8 fusion.44
  295.4 8.3 %all-to-all-done.5 = f32[128,1,512]{2,1,0:T(1,128)} async-done(((f32[128,1,512]{2,1,0:T(1,128)}), f32[128,1,512]{2,1,0:T(1,128)}, u32[]{:S(2)}, u32[]{:S(2)}) %all-to-all-start.5) | async-done | bytes 262176 | tf_op jit(solution)/shard_map/all_to_all | solution.py:66
  305.4 2.9 reshape.166
  308.3 3.0 slice_reduce_fusion
  311.3 2.1 copy.90
  (134 shorter events, 46.7 us)
Async XLA Ops:
  7.2 118.9 %copy-start = (bf16[1,1664,1024]{2,1,0:T(8,128)(2,1)S(1)}, bf16[1,1664,1024]{2,1,0:T(8,128)(2,1)}, u32[]{:S(2)}) copy-start(bf16[1,1664,1024]{2,1,0:T(8,128)(2,1)} %param.16) | copy-start | bytes 10223620
  7.2 12.4 %copy-start.10 = (s32[128,2]{0,1:T(2,128)S(1)}, s32[128,2]{0,1:T(2,128)}, u32[]{:S(2)}) copy-start(s32[128,2]{0,1:T(2,128)} %param.12) | copy-start | bytes 3076
  7.2 112.5 %all-gather.5.cloned.1.call-start = ((), (), s32[]{:S(2)}) async-start(), calls=%async_computation.10 | async-start | bytes 5529600 | tf_op jit(solution)/shard_map/all_gather | solution.py:121
  19.6 1.5 copy-start.18
  24.4 6.7 %copy-start.22 = (pred[128]{0:T(512)(128)(4,1)}, pred[128]{0:T(512)(128)(4,1)S(1)}, u32[]{:S(2)}) copy-start(pred[128]{0:T(512)(128)(4,1)S(1)} %broadcast_in_dim.113) | copy-start | bytes 388
  72.2 100.1 %all-gather.7.cloned.1.call-start = ((), (), s32[]{:S(2)}) async-start(), calls=%async_computation.11 | async-start | bytes 5529600 | tf_op jit(solution)/shard_map/all_gather | solution.py:121
  76.6 1.8 copy-start.8
  111.8 94.8 %reduce-scatter.3.cloned.1.call-start = ((), (), s32[]{:S(2)}) async-start(), calls=%async_computation.8 | async-start | bytes 2867200 | tf_op jit(solution)/shard_map/reduce_scatter | solution.py:143
  120.7 5.3 %copy-start.14 = (bf16[20,32,3456]{2,1,0:T(8,128)(2,1)S(1)}, bf16[20,32,3456]{2,1,0:T(8,128)(2,1)}, u32[]{:S(2)}) copy-start(bf16[20,32,3456]{2,1,0:T(8,128)(2,1)} %all-gather.5.cloned.1.call-done) | copy-start | bytes 13271044
  130.9 2.8 copy-start.27
  135.4 104.5 %reduce-scatter.5.cloned.1.call-start = ((), (), s32[]{:S(2)}) async-start(), calls=%async_computation.9 | async-start | bytes 2867200 | tf_op jit(solution)/shard_map/reduce_scatter | solution.py:143
  173.5 5.3 %copy-start.15 = (bf16[20,32,3456]{2,1,0:T(8,128)(2,1)S(1)}, bf16[20,32,3456]{2,1,0:T(8,128)(2,1)}, u32[]{:S(2)}) copy-start(bf16[20,32,3456]{2,1,0:T(8,128)(2,1)} %all-gather.7.cloned.1.call-done) | copy-start | bytes 13271044
  183.7 2.8 copy-start.25
  186.5 1.7 copy-start.11
  186.5 2.6 copy-start.24
  208.9 33.4 %all-to-all-start.1 = ((bf16[5,32,1792]{2,0,1:T(8,128)(2,1)}), bf16[5,32,1792]{2,0,1:T(8,128)(2,1)S(1)}, u32[]{:S(2)}, u32[]{:S(2)}) async-start(bf16[5,32,1792]{2,0,1:T(8,128)(2,1)} %copy.81), calls=%async_computation.2 | async-start | bytes 1835008 | tf_op jit(solution)/shard_map/all_to_all | solution.py:145
  217.0 10.8 %copy-start.28 = (bf16[640,1024]{1,0:T(8,128)(2,1)S(1)}, bf16[640,1024]{1,0:T(8,128)(2,1)}, u32[]{:S(2)}) copy-start(bf16[640,1024]{1,0:T(8,128)(2,1)} %copy-done.27) | copy-start | bytes 3932164
  234.2 15.8 %copy-start.26 = (bf16[640,1024]{1,0:T(8,128)(2,1)S(1)}, bf16[640,1024]{1,0:T(8,128)(2,1)}, u32[]{:S(2)}) copy-start(bf16[640,1024]{1,0:T(8,128)(2,1)} %copy-done.25) | copy-start | bytes 3932164
  242.3 23.3 %all-to-all-start.3 = ((bf16[5,32,1792]{2,0,1:T(8,128)(2,1)}), bf16[5,32,1792]{2,0,1:T(8,128)(2,1)S(1)}, u32[]{:S(2)}, u32[]{:S(2)}) async-start(bf16[5,32,1792]{2,0,1:T(8,128)(2,1)} %copy.85), calls=%async_computation.5 | async-start | bytes 1835008 | tf_op jit(solution)/shard_map/all_to_all | solution.py:145
  257.6 8.5 %copy-start.6 = (f32[128,320]{0,1:T(8,128)S(1)}, f32[128,320]{0,1:T(8,128)}, u32[]{:S(2)}) copy-start(f32[128,320]{0,1:T(8,128)} %convert_reduce_fusion.3) | copy-start | bytes 491524
  257.7 9.3 %copy-start.19 = (s32[128,2]{0,1:T(2,128)S(1)}, s32[128,2]{0,1:T(2,128)}, u32[]{:S(2)}) copy-start(s32[128,2]{0,1:T(2,128)} %copy-done.18) | copy-start | bytes 3076
  265.7 1.4 copy-start.20
  265.8 1.5 copy-start.4
  265.8 1.8 copy-start.2
  265.8 1.8 copy-start.7
  265.8 1.8 copy-start.9
  265.8 1.8 copy-start.13
  265.8 1.8 copy-start.17
  269.6 23.1 %copy-start.23 = (pred[128]{0:T(512)(128)(4,1)S(1)}, pred[128]{0:T(512)(128)(4,1)}, u32[]{:S(2)}) copy-start(pred[128]{0:T(512)(128)(4,1)} %copy-done.22) | copy-start | bytes 388
  271.4 15.5 %all-to-all-start.4 = ((f32[128,1,512]{2,1,0:T(1,128)}), f32[128,1,512]{2,1,0:T(1,128)S(1)}, u32[]{:S(2)}, u32[]{:S(2)}) async-start(f32[128,1,512]{2,1,0:T(1,128)} %bitcast.20), calls=%async_computation.6 | async-start | bytes 524288 | tf_op jit(solution)/shard_map/all_to_all | solution.py:61
  288.0 15.8 %all-to-all-start.5 = ((f32[128,1,512]{2,1,0:T(1,128)}), f32[128,1,512]{2,1,0:T(1,128)}, u32[]{:S(2)}, u32[]{:S(2)}) async-start(f32[128,1,512]{2,1,0:T(1,128)} %broadcast_in_dim.131), calls=%async_computation.7 | async-start | bytes 524288 | tf_op jit(solution)/shard_map/all_to_all | solution.py:66
  292.7 20.7 %copy-start.1 = (bf16[1,1664,1024]{2,1,0:T(8,128)(2,1)S(1)}, bf16[1,1664,1024]{2,1,0:T(8,128)(2,1)}, u32[]{:S(2)}) copy-start(bf16[1,1664,1024]{2,1,0:T(8,128)(2,1)} %param.16) | copy-start | bytes 10223620
  (5 other events, 4.8 us)
Sparse Core Ops, SparseCore 0:
  72.4 47.2 all-gather.4
  121.9 50.4 all-gather.6
  174.8 31.7 reduce-scatter.2
  208.9 31.0 reduce-scatter.4
